TPU v7x, 32 devices: a whole 2x2x4 slice. The times are simulated.
32 devices in a mesh: grp: 4 (over y, x), leaf: 8 (over z, core).
Axes of the slice: x: 2, y: 2, z: 4, core: 2. Of those that a mesh axis runs over, the one named last changes fastest.
Arguments:
- direction: bfloat16 [49152, 256], P(('grp', 'leaf')), may hold values from -6 to 6
- residual: bfloat16 [49152, 256], P(('grp', 'leaf')), may hold values from -6 to 6
- leaf_order: int32 [32, 1536], P(('grp', 'leaf')), may hold values from 0 to 1535, as said below
- diag_block: bfloat16 [32, 1536, 1536], P(('grp', 'leaf')), may hold values from -0.15625 to 0.15625
- up_basis: bfloat16 [32, 1536, 128], P(('grp', 'leaf')), may hold values from -0.15625 to 0.15625
- down_basis: bfloat16 [32, 1536, 128], P(('grp', 'leaf')), may hold values from -0.5 to 0.5
- leaf_ops: bfloat16 [3, 32, 128, 128], P(None, ('grp', 'leaf')), may hold values from -0.375 to 0.375
- inner_ops: bfloat16 [3, 24, 128, 128], P(None, 'grp'), may hold values from -0.375 to 0.375
- top_ops: bfloat16 [3, 6, 128, 128], replicated, may hold values from -0.375 to 0.375
- ridge_shift: float32 [1], replicated, may hold values from 0.5 to 2
Outputs:
- image: bfloat16 [49152, 256], P(('grp', 'leaf'))
- curvature_gram: float32 [256, 256], replicated
- residual_gram: float32 [256, 256], replicated
Inputs may be any that keep to these rules, and one draw needn't show every extreme that they name: Each row of leaf_order is a permutation of 0 to 1535.
All inputs are finite; a program needn't handle non-finite values.
Results may differ from a plain program's by a relative error of at most 0.022.
Values may be sent and summed in bfloat16 or wider, within the bound.
No kernel may reach another device: no remote copies, remote signals or barrier semaphores. Data moves between devices by JAX's collectives and lax.ppermute only.
A program may use at most 64 MiB of HBM per device.

v0:
```python
import jax
import jax.numpy as jnp
from jax import lax
from jax.sharding import PartitionSpec as P


def from_partner(block, axis, apart):
    count = lax.axis_size(axis)
    route = []
    for low in range(count):
        high = low | 1 << apart
        if high != low and high < count:
            route += [(low, high), (high, low)]
    return lax.ppermute(block, axis, route)


def lift_single(transfer, skeleton):
    return jnp.einsum("rs,rk->sk", transfer, skeleton, preferred_element_type=jnp.float32).astype(
        jnp.bfloat16
    )


def body(
    direction,
    residual,
    leaf_order,
    diag_block,
    up_basis,
    down_basis,
    leaf_ops,
    inner_ops,
    top_ops,
    ridge_shift,
):
    leaves_here = lax.axis_size("leaf")
    groups = lax.axis_size("grp")
    leaf_levels = leaves_here.bit_length() - 1
    group_levels = groups.bit_length() - 1
    total_levels = leaf_levels + group_levels
    my_leaf = lax.axis_index("leaf")
    my_group = lax.axis_index("grp")
    ordering = leaf_order[0]
    ordered = jnp.take(direction, ordering, axis=0)
    skeleton = jnp.einsum(
        "nr,nk->rk", up_basis[0], ordered, preferred_element_type=jnp.float32
    ).astype(jnp.bfloat16)

    def inner_offset(height):
        return sum((leaves_here >> section for section in range(1, height)))

    def top_offset(upper_level):
        return sum((groups >> section for section in range(upper_level)))

    def path_operators(height):
        if height == 0:
            return leaf_ops[:, 0]
        if height < leaf_levels:
            return lax.dynamic_index_in_dim(
                inner_ops, inner_offset(height) + (my_leaf >> height), 1, keepdims=False
            )
        upper_level = height - leaf_levels
        return lax.dynamic_index_in_dim(
            top_ops, top_offset(upper_level) + (my_group >> upper_level), 1, keepdims=False
        )

    contrib = lift_single(leaf_ops[0, 0], skeleton)
    siblings = []
    for bit_index in range(leaf_levels):
        other_skeleton, other_contrib = from_partner((skeleton, contrib), "leaf", bit_index)
        siblings.append(other_skeleton)
        skeleton = (contrib.astype(jnp.float32) + other_contrib.astype(jnp.float32)).astype(
            jnp.bfloat16
        )
        contrib = lift_single(path_operators(bit_index + 1)[0], skeleton)
    for bit_index in range(group_levels):
        other_skeleton, other_contrib = from_partner((skeleton, contrib), "grp", bit_index)
        siblings.append(other_skeleton)
        if bit_index + 1 < group_levels:
            skeleton = (contrib.astype(jnp.float32) + other_contrib.astype(jnp.float32)).astype(
                jnp.bfloat16
            )
            contrib = lift_single(path_operators(leaf_levels + bit_index + 1)[0], skeleton)
    coarse = jnp.zeros((up_basis.shape[2], direction.shape[1]), jnp.bfloat16)
    for height in reversed(range(total_levels)):
        operators = path_operators(height)
        coupled = jnp.dot(operators[2], siblings[height], preferred_element_type=jnp.float32)
        passed = jnp.dot(operators[1], coarse, preferred_element_type=jnp.float32)
        coarse = (coupled + passed).astype(jnp.bfloat16)
    local = jnp.dot(diag_block[0], ordered, preferred_element_type=jnp.float32)
    local = local + jnp.dot(down_basis[0], coarse, preferred_element_type=jnp.float32)
    restored = jnp.zeros(local.shape, jnp.float32).at[ordering].set(local)
    image = (restored + ridge_shift[0] * direction.astype(jnp.float32)).astype(jnp.bfloat16)
    curvature_part = jnp.einsum("nk,nm->km", direction, image, preferred_element_type=jnp.float32)
    correlation_part = jnp.einsum("nk,nm->km", residual, image, preferred_element_type=jnp.float32)
    curvature, correlation = lax.psum((curvature_part, correlation_part), ("grp", "leaf"))
    points_total = direction.shape[0] * leaves_here * groups
    return (image, curvature / points_total, correlation / points_total)


def solution(mesh):
    return jax.shard_map(
        body,
        mesh=mesh,
        in_specs=(
            P(("grp", "leaf"), None),
            P(("grp", "leaf"), None),
            P(("grp", "leaf"), None),
            P(("grp", "leaf"), None, None),
            P(("grp", "leaf"), None, None),
            P(("grp", "leaf"), None, None),
            P(None, ("grp", "leaf"), None, None),
            P(None, "grp", None, None),
            P(),
            P(),
        ),
        out_specs=(P(("grp", "leaf"), None), P(), P()),
        check_vma=False,
    )
```

profile of v0, /device:TPU:0, one launch (start us, length us, event | category | flops | bytes accessed | tf_op | source)
XLA Modules:
  0.0 201.7 jit_solution(530703202432133354)
XLA Ops:
  7.2 0.8 fusion.27
  8.0 0.7 reduce.1
  8.8 4.9 %gather_fusion = bf16[1536,256]{1,0:T(8,128)(2,1)S(1)} fusion(bf16[1536,256]{1,0:T(8,128)(2,1)} %param.10, s32[2048]{0:T(1024)S(1)} %pad_clamp_fusion), kind=kCustom, calls=%fused_computation | custom fusion | bytes 1579008 | tf_op jit(solution)/shard_map/jit(_take)/gather | solution.py:43
  13.7 0.7 convolution_convert_fusion
  15.3 0.9 collective-permute-done.1
  16.2 1.0 convolution_convert_fusion.3
  17.2 3.0 %collective-permute-start.3 = (bf16[128,256]{1,0:T(8,128)(2,1)S(1)}, bf16[128,256]{1,0:T(8,128)(2,1)S(1)}, u32[]{:S(2)}, u32[]{:S(2)}) collective-permute-start(bf16[128,256]{1,0:T(8,128)(2,1)S(1)} %convolution_convert_fusion.3), channel_id=1, source_target_pairs={{0,2},{2,0},{1,3},{3,1},{4,6},{6,4},{5,7},{7,5},{8,10},{10,8},{9,1... | collective-permute-start | bytes 196616 | tf_op jit(solution)/shard_map/ppermute | solution.py:14
  20.2 2.4 %collective-permute-done.3 = bf16[128,256]{1,0:T(8,128)(2,1)S(1)} collective-permute-done((bf16[128,256]{1,0:T(8,128)(2,1)S(1)}, bf16[128,256]{1,0:T(8,128)(2,1)S(1)}, u32[]{:S(2)}, u32[]{:S(2)}) %collective-permute-start.3) | collective-permute-done | bytes 65568 | tf_op jit(solution)/shard_map/ppermute | solution.py:14
  22.6 1.0 convolution_convert_fusion.2
  23.6 2.9 %collective-permute-start.5 = (bf16[128,256]{1,0:T(8,128)(2,1)S(1)}, bf16[128,256]{1,0:T(8,128)(2,1)S(1)}, u32[]{:S(2)}, u32[]{:S(2)}) collective-permute-start(bf16[128,256]{1,0:T(8,128)(2,1)S(1)} %convolution_convert_fusion.2), channel_id=1, source_target_pairs={{0,4},{4,0},{1,5},{5,1},{2,6},{6,2},{3,7},{7,3},{8,12},{12,8},{9,1... | collective-permute-start | bytes 196616 | tf_op jit(solution)/shard_map/ppermute | solution.py:14
  26.5 2.3 %collective-permute-done.5 = bf16[128,256]{1,0:T(8,128)(2,1)S(1)} collective-permute-done((bf16[128,256]{1,0:T(8,128)(2,1)S(1)}, bf16[128,256]{1,0:T(8,128)(2,1)S(1)}, u32[]{:S(2)}, u32[]{:S(2)}) %collective-permute-start.5) | collective-permute-done | bytes 65568 | tf_op jit(solution)/shard_map/ppermute | solution.py:14
  28.9 1.0 convolution_convert_fusion.1
  29.8 1.8 collective-permute-start.7
  31.6 5.3 %fusion = f32[256,1536]{1,0:T(8,128)} fusion(bf16[1,1536,1536]{2,1,0:T(8,128)(2,1)} %param.13, bf16[1536,256]{1,0:T(8,128)(2,1)S(1)} %gather_fusion, pred[1536]{0:T(1024)(128)(4,1)S(1)} %compare_and_fusion), kind=kOutput, calls=%fused_computation.2 | convolution fusion | flops 1208352768 | bytes 7079424 | tf_op jit(solution)/shard_map/dot_general | solution.py:89
  37.6 1.6 collective-permute-start.8
  39.2 0.9 fusion.17
  40.1 1.6 collective-permute-start.2
  41.7 3.2 %collective-permute-start.4 = (bf16[128,256]{1,0:T(8,128)(2,1)S(1)}, bf16[128,256]{1,0:T(8,128)(2,1)S(1)}, u32[]{:S(2)}, u32[]{:S(2)}) collective-permute-start(bf16[128,256]{1,0:T(8,128)(2,1)S(1)} %add_convert_fusion.3), channel_id=1, source_target_pairs={{0,4},{4,0},{1,5},{5,1},{2,6},{6,2},{3,7},{7,3},{8,12},{12,8},{9,1... | collective-permute-start | bytes 196616 | tf_op jit(solution)/shard_map/ppermute | solution.py:14
  45.4 1.1 fusion.9
  46.5 2.6 %collective-permute-done.6 = bf16[128,256]{1,0:T(8,128)(2,1)S(1)} collective-permute-done((bf16[128,256]{1,0:T(8,128)(2,1)S(1)}, bf16[128,256]{1,0:T(8,128)(2,1)S(1)}, u32[]{:S(2)}, u32[]{:S(2)}) %collective-permute-start.6) | collective-permute-done | bytes 65568 | tf_op jit(solution)/shard_map/ppermute | solution.py:14
  49.1 1.1 fusion.10
  50.2 1.1 fusion.11
  51.3 1.1 fusion.12
  52.5 1.9 fusion.2
  54.4 1.6 copy.16
  56.0 7.8 %scatter_custom_fusion = f32[1536,256]{1,0:T(8,128)S(1)} fusion(s32[1536]{0:T(1024)S(1)} %fusion.27, f32[1536,256]{1,0:T(8,128)} %copy.16, f32[]{:T(128)} %constant.47.clone.1), kind=kCustom, calls=%fused_computation.29 | custom fusion | bytes 1573376 | tf_op jit(solution)/shard_map/scatter | solution.py:91
  64.1 1.1 convolution_bitcast_fusion.1
  65.2 1.1 convolution_bitcast_fusion
  66.3 125.8 %all-reduce.3.cloned.1.call-done = (f32[256,256]{0,1:T(8,128)}, f32[256,256]{0,1:T(8,128)}) async-done(((f32[256,256]{0,1:T(8,128)}, f32[256,256]{0,1:T(8,128)}), (f32[256,256]{0,1:T(8,128)}, f32[256,256]{0,1:T(8,128)})) %all-reduce.3.cloned.1.call-update) | async-done | bytes 524304 | tf_op jit(solution)/shard_map/psum | solution.py:95
  192.1 1.1 broadcast_multiply_fusion
  193.2 0.8 copy.17
  194.0 0.8 copy.18
  (30 shorter events, 1.8 us)
Async XLA Ops:
  7.2 58.0 %copy-start = (bf16[1536,256]{1,0:T(8,128)(2,1)S(1)}, bf16[1536,256]{1,0:T(8,128)(2,1)}, u32[]{:S(2)}) copy-start(bf16[1536,256]{1,0:T(8,128)(2,1)} %param.11) | copy-start | bytes 2359300
  7.2 184.9 %all-reduce.3.cloned.1.call-start = ((), (), s32[]{:S(2)}) async-start(), calls=%async_computation | async-start | bytes 1048576 | tf_op jit(solution)/shard_map/psum | solution.py:95
  8.8 5.0 %copy-start.5 = (bf16[1,1536,128]{2,1,0:T(8,128)(2,1)S(1)}, bf16[1,1536,128]{2,1,0:T(8,128)(2,1)}, u32[]{:S(2)}) copy-start(bf16[1,1536,128]{2,1,0:T(8,128)(2,1)} %param.14) | copy-start | bytes 1179652
  13.7 0.9 copy-start.4
  14.8 1.5 collective-permute-start.1
  17.2 5.4 %collective-permute-start.3 = (bf16[128,256]{1,0:T(8,128)(2,1)S(1)}, bf16[128,256]{1,0:T(8,128)(2,1)S(1)}, u32[]{:S(2)}, u32[]{:S(2)}) collective-permute-start(bf16[128,256]{1,0:T(8,128)(2,1)S(1)} %convolution_convert_fusion.3), channel_id=1, source_target_pairs={{0,2},{2,0},{1,3},{3,1},{4,6},{6,4},{5,7},{7,5},{8,10},{10,8},{9,1... | collective-permute-start | bytes 196616 | tf_op jit(solution)/shard_map/ppermute | solution.py:14
  23.6 5.3 %collective-permute-start.5 = (bf16[128,256]{1,0:T(8,128)(2,1)S(1)}, bf16[128,256]{1,0:T(8,128)(2,1)S(1)}, u32[]{:S(2)}, u32[]{:S(2)}) collective-permute-start(bf16[128,256]{1,0:T(8,128)(2,1)S(1)} %convolution_convert_fusion.2), channel_id=1, source_target_pairs={{0,4},{4,0},{1,5},{5,1},{2,6},{6,2},{3,7},{7,3},{8,12},{12,8},{9,1... | collective-permute-start | bytes 196616 | tf_op jit(solution)/shard_map/ppermute | solution.py:14
  26.5 25.9 %collective-permute-start = (bf16[128,256]{0,1:T(8,128)(2,1)S(1)}, bf16[128,256]{0,1:T(8,128)(2,1)S(1)}, u32[]{:S(2)}, u32[]{:S(2)}) collective-permute-start(bf16[128,256]{0,1:T(8,128)(2,1)S(1)} %bitcast.82), channel_id=1, source_target_pairs={{0,1},{1,0},{2,3},{3,2},{4,5},{5,4},{6,7},{7,6},{8,9},{9,8},{10,11... | collective-permute-start | bytes 196616 | tf_op jit(solution)/shard_map/ppermute | solution.py:14
  29.8 7.8 %collective-permute-start.7 = (bf16[128,256]{1,0:T(8,128)(2,1)S(1)}, bf16[128,256]{1,0:T(8,128)(2,1)S(1)}, u32[]{:S(2)}, u32[]{:S(2)}) collective-permute-start(bf16[128,256]{1,0:T(8,128)(2,1)S(1)} %convolution_convert_fusion.1), channel_id=1, source_target_pairs={{0,8},{8,0},{16,24},{24,16},{1,9},{9,1},{17,25},{25,17},{2,10},{10... | collective-permute-start | bytes 196616 | tf_op jit(solution)/shard_map/ppermute | solution.py:14
  36.9 15.6 %copy-start.3 = (bf16[1,1536,128]{2,1,0:T(8,128)(2,1)S(1)}, bf16[1,1536,128]{2,1,0:T(8,128)(2,1)}, u32[]{:S(2)}) copy-start(bf16[1,1536,128]{2,1,0:T(8,128)(2,1)} %param.15) | copy-start | bytes 1179652
  37.6 7.8 %collective-permute-start.8 = (bf16[128,256]{1,0:T(8,128)(2,1)S(1)}, bf16[128,256]{1,0:T(8,128)(2,1)S(1)}, u32[]{:S(2)}, u32[]{:S(2)}) collective-permute-start(bf16[128,256]{1,0:T(8,128)(2,1)S(1)} %add_convert_fusion.1), channel_id=1, source_target_pairs={{0,16},{16,0},{8,24},{24,8},{1,17},{17,1},{9,25},{25,9},{2,18},{18... | collective-permute-start | bytes 196616 | tf_op jit(solution)/shard_map/ppermute | solution.py:14
  40.1 11.2 %collective-permute-start.2 = (bf16[128,256]{0,1:T(8,128)(2,1)S(1)}, bf16[128,256]{0,1:T(8,128)(2,1)S(1)}, u32[]{:S(2)}, u32[]{:S(2)}) collective-permute-start(bf16[128,256]{0,1:T(8,128)(2,1)S(1)} %add_convert_fusion.4), channel_id=1, source_target_pairs={{0,2},{2,0},{1,3},{3,1},{4,6},{6,4},{5,7},{7,5},{8,10},{10,8},{9,1... | collective-permute-start | bytes 196616 | tf_op jit(solution)/shard_map/ppermute | solution.py:14
  41.7 8.5 %collective-permute-start.4 = (bf16[128,256]{1,0:T(8,128)(2,1)S(1)}, bf16[128,256]{1,0:T(8,128)(2,1)S(1)}, u32[]{:S(2)}, u32[]{:S(2)}) collective-permute-start(bf16[128,256]{1,0:T(8,128)(2,1)S(1)} %add_convert_fusion.3), channel_id=1, source_target_pairs={{0,4},{4,0},{1,5},{5,1},{2,6},{6,2},{3,7},{7,3},{8,12},{12,8},{9,1... | collective-permute-start | bytes 196616 | tf_op jit(solution)/shard_map/ppermute | solution.py:14
  44.8 4.3 %collective-permute-start.6 = (bf16[128,256]{1,0:T(8,128)(2,1)S(1)}, bf16[128,256]{1,0:T(8,128)(2,1)S(1)}, u32[]{:S(2)}, u32[]{:S(2)}) collective-permute-start(bf16[128,256]{1,0:T(8,128)(2,1)S(1)} %add_convert_fusion.2), channel_id=1, source_target_pairs={{0,8},{8,0},{16,24},{24,16},{1,9},{9,1},{17,25},{25,17},{2,10},{10... | collective-permute-start | bytes 196616 | tf_op jit(solution)/shard_map/ppermute | solution.py:14
  56.0 7.8 %copy-start.1 = (bf16[1536,256]{1,0:T(8,128)(2,1)S(1)}, bf16[1536,256]{1,0:T(8,128)(2,1)}, u32[]{:S(2)}) copy-start(bf16[1536,256]{1,0:T(8,128)(2,1)} %param.10) | copy-start | bytes 2359300
  64.0 1.1 copy-start.2
Sparse Core Ops, SparseCore 0:
  66.4 125.6 all-reduce.2
where the time goes:
time: 203 us; the launch traced here: 202 us
  waiting for transfers between devices  134 us (66%)
  matrix products  18.4 us (9%)
  local copies, waits for them, and re-layouts  16.2 us (8%)
  starting transfers between devices  15.2 us (7%)
  between operations  14.9 us (7%)
  other arithmetic  2.88 us (1%)
    psum x1, waiting for transfers between devices, body(): lax.psum((curvature_part, correlation_part), ('grp', 'leaf'))  126 us
    ppermute x9, starting transfers between devices, from_partner(): return lax.ppermute(block, axis, route)  15.1 us
    ppermute x9, waiting for transfers between devices, from_partner(): return lax.ppermute(block, axis, route)  8.29 us
    scatter x1, local copies, waits for them, and re-layouts, body(): restored = jnp.zeros(local.shape, jnp.float32).at[ordering].set(local)  7.8 us
    dot_general x5, matrix products, body(): passed = jnp.dot(operators[1], coarse, preferred_element_type=jnp.float32)  5.26 us
    dot_general x1, matrix products, body(): local = jnp.dot(diag_block[0], ordered, preferred_element_type=jnp.float32)  5.26 us
    gather x1, local copies, waits for them, and re-layouts, body(): ordered = jnp.take(direction, ordering, axis=0)  4.93 us
  transfers between devices with their start and end apart: 10, of which 5 were waited for; matrix products, arithmetic and copies ran while one was open for 6% of the time, Pallas kernels for 0%

commit v1 on v0

v1 whole, which is shorter than its diff:
```python
import jax
import jax.numpy as jnp
from jax import lax
from jax.sharding import PartitionSpec as P

BF = jnp.bfloat16
F32 = jnp.float32


def swap(block, axis, apart):
    count = lax.axis_size(axis)
    return lax.ppermute(block, axis, [(i, i ^ (1 << apart)) for i in range(count)])


def mm(a, b):
    return lax.dot_general(a, b, (((1,), (0,)), ((), ())), preferred_element_type=F32)


def mmt(a, b):
    return lax.dot_general(a, b, (((1,), (1,)), ((), ())), preferred_element_type=F32)


def cut(x, which, size, axis=0):
    return lax.dynamic_slice_in_dim(x, which * size, size, axis)


def join(bit, own, other, axis=0):
    low = jnp.where(bit == 0, own, other)
    high = jnp.where(bit == 0, other, own)
    return jnp.concatenate([low, high], axis)


def body(
    direction,
    residual,
    leaf_order,
    diag_block,
    up_basis,
    down_basis,
    leaf_ops,
    inner_ops,
    top_ops,
    ridge_shift,
):
    leaves_here = lax.axis_size("leaf")
    groups = lax.axis_size("grp")
    leaf_levels = leaves_here.bit_length() - 1
    group_levels = groups.bit_length() - 1
    total_levels = leaf_levels + group_levels
    my_leaf = lax.axis_index("leaf")
    my_group = lax.axis_index("grp")
    points, nrhs = direction.shape
    half = nrhs // 2
    core = my_leaf & 1
    ridge = ridge_shift[0]

    def node_ops(height, flip):
        if height < leaf_levels:
            start = sum(leaves_here >> s for s in range(1, height))
            node = start + ((my_leaf >> height) ^ flip)
            return lax.dynamic_index_in_dim(inner_ops, node, 1, keepdims=False)
        upper = height - leaf_levels
        start = sum(groups >> s for s in range(upper))
        node = start + ((my_group >> upper) ^ flip)
        return lax.dynamic_index_in_dim(top_ops, node, 1, keepdims=False)

    both = jnp.concatenate([direction, residual], 1)
    rows = lax.broadcasted_iota(jnp.int32, (points, points), 0)
    spread = (rows == leaf_order[0][None, :]).astype(BF)
    ordered = lax.dot_general(both, spread, (((0,), (0,)), ((), ())), preferred_element_type=F32).astype(BF)
    st = mm(ordered[:nrhs], up_basis[0]).astype(BF)
    vt = mm(ordered, down_basis[0]).astype(BF)
    up0, down0, cross0 = leaf_ops[0, 0], leaf_ops[1, 0], leaf_ops[2, 0]
    lift = mm(st, up0).astype(BF)
    vr = mm(vt, down0).astype(BF)
    vb = mm(vt, cross0).astype(BF)
    message = jnp.concatenate([st, cut(lift, 1 - core, half), vr, vb], 0)
    got = swap(message, "leaf", 0)
    dense = mmt(diag_block[0], ordered[:nrhs])
    gram = mm(ordered, dense.astype(BF)) + ridge * lax.dot_general(
        both, direction, (((0,), (0,)), ((), ())), preferred_element_type=F32
    )
    got_gram = swap(cut(gram, 1 - core, half, 1).astype(BF), "leaf", 0)
    leaf_sibling = got[:nrhs]
    got_lift = got[nrhs : nrhs + half]
    got_vr = got[nrhs + half : 3 * nrhs + half]
    got_vb = got[3 * nrhs + half :]
    s = (cut(lift, core, half).astype(F32) + got_lift.astype(F32)).astype(BF)
    v = (vr.astype(F32) + got_vr.astype(F32)).astype(BF)
    g = (
        cut(gram, core, half, 1)
        + got_gram.astype(F32)
        + (mmt(vb, cut(leaf_sibling, core, half)) + mmt(got_vb, cut(st, core, half)))
    )
    siblings = {}
    for height in range(1, total_levels):
        own_ops = node_ops(height, 0)
        sib_ops = node_ops(height, 1)
        scatter = height < leaf_levels
        if scatter:
            bit = (my_leaf >> height) & 1
            part = v.shape[0] // 2
            send_v, send_g = cut(v, 1 - bit, part), cut(g, 1 - bit, part).astype(BF)
            v, g = cut(v, bit, part), cut(g, bit, part)
            got = swap(jnp.concatenate([s, send_v, send_g], 0), "leaf", height)
        else:
            part = v.shape[0]
            send_g = g.astype(BF)
            g = send_g.astype(F32)
            got = swap(jnp.concatenate([s, v, send_g], 0), "grp", height - leaf_levels)
        s2, v2, g2 = got[:half], got[half : half + part], got[half + part :]
        siblings[height] = s2
        g = (g + g2.astype(F32)) + (
            mmt(mm(v, own_ops[2]).astype(BF), s2) + mmt(mm(v2, sib_ops[2]).astype(BF), s)
        )
        if height + 1 < total_levels:
            s = (mm(s, own_ops[0]) + mm(s2, sib_ops[0])).astype(BF)
            v = (mm(v, own_ops[1]) + mm(v2, sib_ops[1])).astype(BF)
    coarse = None
    for height in reversed(range(1, total_levels)):
        own_ops = node_ops(height, 0)
        term = mmt(siblings[height], own_ops[2])
        if coarse is not None:
            term = term + mmt(coarse, own_ops[1])
        coarse = term.astype(BF)
    coarse = join(core, coarse, swap(coarse, "leaf", 0))
    leaf_coarse = (mmt(leaf_sibling, cross0) + mmt(coarse, down0)).astype(BF)
    local = dense + mmt(down_basis[0], leaf_coarse)
    restored = mm(spread, local.astype(BF))
    image = (restored + ridge * direction.astype(F32)).astype(BF)
    piece = g.astype(BF)
    for height in reversed(range(1, leaf_levels)):
        piece = join((my_leaf >> height) & 1, piece, swap(piece, "leaf", height))
    piece = join(core, piece, swap(piece, "leaf", 0), 1)
    grams = piece.astype(F32) / (points * leaves_here * groups)
    return image, grams[:nrhs], grams[nrhs:]


def solution(mesh):
    return jax.shard_map(
        body,
        mesh=mesh,
        in_specs=(
            P(("grp", "leaf"), None),
            P(("grp", "leaf"), None),
            P(("grp", "leaf"), None),
            P(("grp", "leaf"), None, None),
            P(("grp", "leaf"), None, None),
            P(("grp", "leaf"), None, None),
            P(None, ("grp", "leaf"), None, None),
            P(None, "grp", None, None),
            P(),
            P(),
        ),
        out_specs=(P(("grp", "leaf"), None), P(), P()),
        check_vma=False,
    )
```

time: 203 us -> 79.3 us (0.39)
  waiting for transfers between devices: 134 us -> 12.3 us
  matrix products: 18.4 us -> 38.8 us
  between operations: 14.9 us -> 1.79 us
  local copies, waits for them, and re-layouts: 16.2 us -> 5.87 us
  other arithmetic: 2.88 us -> 5.67 us
    psum x1 -> x0, waiting for transfers between devices: 126 us -> none  [body(): lax.psum((curvature_part, correlation_part), ('grp', 'leaf'))]
    dot_general x14 -> x38, matrix products: 18.4 us -> 38.8 us  [the longest x17 20.4 us: mmt(): lax.dot_general(a, b, (((1,), (1,)), ((), ())), preferred_element_type=F32)]
    scatter x1 -> x0, local copies, waits for them, and re-layouts: 7.8 us -> none  [body(): restored = jnp.zeros(local.shape, jnp.float32).at[ordering].set(local)]
    gather x1 -> x0, local copies, waits for them, and re-layouts: 4.93 us -> none  [body(): ordered = jnp.take(direction, ordering, axis=0)]
    ppermute x9 -> x10, waiting for transfers between devices: 8.29 us -> 12.3 us  [swap(): lax.ppermute(block, axis, [(i, i ^ 1 << apart) for i in range(count)])]
    concatenate x0 -> x7, other arithmetic: none -> 2.11 us  [the longest x1 0.76 us: body(): message = jnp.concatenate([st, cut(lift, 1 - core, half), vr, vb], 0)]
    ppermute x9 -> x10, starting transfers between devices: 15.1 us -> 13.5 us  [swap(): lax.ppermute(block, axis, [(i, i ^ 1 << apart) for i in range(count)])]
  transfers between devices with their start and end apart: 10 -> 10, of which waited for: 5 -> 5; matrix products, arithmetic and copies ran while one was open for 6% -> 32% of each run, Pallas kernels for 0% -> 0%
where the time goes in v1:
time: 79.3 us; the launch traced here: 77.9 us
  matrix products  38.8 us (49%)
  starting transfers between devices  13.5 us (17%)
  waiting for transfers between devices  12.3 us (16%)
  local copies, waits for them, and re-layouts  5.87 us (7%)
  other arithmetic  5.67 us (7%)
  between operations  1.79 us (2%)
    dot_general x17, matrix products, mmt(): lax.dot_general(a, b, (((1,), (1,)), ((), ())), preferred_element_type=F32)  20.4 us
    ppermute x10, starting transfers between devices, swap(): lax.ppermute(block, axis, [(i, i ^ 1 << apart) for i in range(count)])  13.5 us
    ppermute x10, waiting for transfers between devices, swap(): lax.ppermute(block, axis, [(i, i ^ 1 << apart) for i in range(count)])  12.3 us
    dot_general x19, matrix products, mm(): lax.dot_general(a, b, (((1,), (0,)), ((), ())), preferred_element_type=F32)  12.2 us
    dot_general x1, matrix products, body(): lax.dot_general(both, spread, (((0,), (0,)), ((), ())), preferred_element...  4.19 us
    unnamed x33, local copies, waits for them, and re-layouts  3.13 us
    dot_general x1, matrix products, body(): lax.dot_general(both, direction, (((0,), (0,)), ((), ())), preferred_elem...  2.02 us
    select_n x4, other arithmetic, join(): low = jnp.where(bit == 0, own, other)  1.77 us
  transfers between devices with their start and end apart: 10, of which 5 were waited for; matrix products, arithmetic and copies ran while one was open for 32% of the time, Pallas kernels for 0%

profile of v1, /device:TPU:0, one launch (start us, length us, event | category | flops | bytes accessed | tf_op | source)
XLA Modules:
  0.0 77.9 jit_solution(11254678682343607448)
XLA Ops:
  0.7 2.2 %constant_dynamic-update-slice_fusion.1 = bf16[1536,512]{1,0:T(8,128)(2,1)} fusion(bf16[1536,256]{1,0:T(8,128)(2,1)} %param.10), kind=kLoop, calls=%fused_computation.189 | loop fusion | bytes 1572864
  2.9 1.0 %constant_dynamic-update-slice_fusion = bf16[1536,512]{1,0:T(8,128)(2,1)} fusion(bf16[1536,512]{1,0:T(8,128)(2,1)} %constant_dynamic-update-slice_fusion.1, bf16[1536,256]{1,0:T(8,128)(2,1)S(1)} %copy-done.3), kind=kLoop, calls=%fused_computation.188 | loop fusion | bytes 1572864 | tf_op jit(solution)/shard_map/concatenate | solution.py:67
  3.9 4.2 %fusion.6 = bf16[512,1536]{1,0:T(8,128)(2,1)S(1)} fusion(bf16[1536,512]{1,0:T(8,128)(2,1)} %constant_dynamic-update-slice_fusion, s32[1536]{0:T(1024)S(1)} %reduce), kind=kOutput, calls=%fused_computation.7 | convolution fusion | flops 2419064832 | bytes 3151872 | tf_op jit(solution)/shard_map/dot_general | solution.py:70
  11.2 3.7 %fusion.2 = f32[256,1536]{1,0:T(8,128)S(1)} fusion(bf16[1,1536,1536]{2,1,0:T(8,128)(2,1)} %param.13, bf16[512,1536]{1,0:T(8,128)(2,1)S(1)} %fusion.6), kind=kOutput, calls=%fused_computation.3 | convolution fusion | flops 1207959552 | bytes 7077888 | tf_op jit(solution)/shard_map/dot_general | solution.py:20
  16.8 2.0 %fusion.10 = f32[512,256]{1,0:T(8,128)S(1)} fusion(f32[512,256]{1,0:T(8,128)S(1)} %fusion.28, bf16[1536,512]{1,0:T(8,128)(2,1)} %constant_dynamic-update-slice_fusion, bf16[1536,256]{1,0:T(8,128)(2,1)S(1)} %copy-done.4, f32[]{:T(128)} %bitcast.126), kind=kOutput, calls=%fused_computation.13 | convolution fusion | flops 402915328 | bytes 3407876 | tf_op jit(solution)/shard_map/dot_general | solution.py:80
  19.8 1.1 %fusion.36 = f32[512,128]{1,0:T(8,128)S(1)} fusion(bf16[1408,128]{1,0:T(8,128)(2,1)} %collective-permute-done, bf16[256,128]{1,0:T(8,128)(2,1)S(1)} %convolution_convert_fusion.3, s32[]{:T(128)S(6)} %select_n.103), kind=kOutput, calls=%fused_computation.73 | convolution fusion | flops 16777216 | bytes 425988 | tf_op jit(solution)/shard_map/dot_general | solution.py:20
  21.1 0.9 %add_convert_fusion = bf16[512,128]{1,0:T(8,128)(2,1)S(1)} fusion(bf16[512,128]{1,0:T(8,128)(2,1)S(1)} %convolution_convert_fusion.1, bf16[1408,128]{1,0:T(8,128)(2,1)} %collective-permute-done), kind=kLoop, calls=%fused_computation.71 | loop fusion | flops 262144 | bytes 393216 | tf_op jit(solution)/shard_map/convert_element_type | solution.py:89
  22.9 3.1 %collective-permute-start.2 = (bf16[640,128]{1,0:T(8,128)(2,1)S(1)}, bf16[640,128]{1,0:T(8,128)(2,1)S(1)}, u32[]{:S(2)}, u32[]{:S(2)}) collective-permute-start(bf16[640,128]{1,0:T(8,128)(2,1)S(1)} %pad_maximum_fusion.1), channel_id=1, source_target_pairs={{0,2},{1,3},{2,0},{3,1},{4,6},{5,7},{6,4},{7,5},{8,10},{9,11},{10,... | collective-permute-start | bytes 491528 | tf_op jit(solution)/shard_map/ppermute | solution.py:12
  26.2 4.2 %collective-permute-done.2 = bf16[640,128]{1,0:T(8,128)(2,1)S(1)} collective-permute-done((bf16[640,128]{1,0:T(8,128)(2,1)S(1)}, bf16[640,128]{1,0:T(8,128)(2,1)S(1)}, u32[]{:S(2)}, u32[]{:S(2)}) %collective-permute-start.2) | collective-permute-done | bytes 163872 | tf_op jit(solution)/shard_map/ppermute | solution.py:12
  31.5 2.8 %collective-permute-start.3 = (bf16[384,128]{1,0:T(8,128)(2,1)S(1)}, bf16[384,128]{1,0:T(8,128)(2,1)S(1)}, u32[]{:S(2)}, u32[]{:S(2)}) collective-permute-start(bf16[384,128]{1,0:T(8,128)(2,1)S(1)} %pad_maximum_fusion.3), channel_id=1, source_target_pairs={{0,4},{1,5},{2,6},{3,7},{4,0},{5,1},{6,2},{7,3},{8,12},{9,13},{10,... | collective-permute-start | bytes 294920 | tf_op jit(solution)/shard_map/ppermute | solution.py:12
  34.6 4.2 %collective-permute-done.3 = bf16[384,128]{1,0:T(8,128)(2,1)S(1)} collective-permute-done((bf16[384,128]{1,0:T(8,128)(2,1)S(1)}, bf16[384,128]{1,0:T(8,128)(2,1)S(1)}, u32[]{:S(2)}, u32[]{:S(2)}) %collective-permute-start.3) | collective-permute-done | bytes 98336 | tf_op jit(solution)/shard_map/ppermute | solution.py:12
  39.6 1.4 %collective-permute-start.4 = (bf16[384,128]{1,0:T(8,128)(2,1)S(1)}, bf16[384,128]{1,0:T(8,128)(2,1)S(1)}, u32[]{:S(2)}, u32[]{:S(2)}) collective-permute-start(bf16[384,128]{1,0:T(8,128)(2,1)S(1)} %pad_maximum_fusion.4), channel_id=1, source_target_pairs={{0,8},{8,0},{16,24},{24,16},{1,9},{9,1},{17,25},{25,17},{2,10},{10... | collective-permute-start | bytes 294920 | tf_op jit(solution)/shard_map/ppermute | solution.py:12
  41.0 1.5 %fusion.87 = f32[128,128]{1,0:T(8,128)} fusion(bf16[128,128]{1,0:T(8,128)(2,1)S(1)} %fusion.18, bf16[3,6,128,128]{3,2,1,0:T(8,128)(2,1)} %param.18, s32[]{:T(128)S(6)} %add.218, s32[]{:T(128)S(6)} %select_n.112), kind=kOutput, calls=%fused_computation.149 | convolution fusion | flops 4194304 | bytes 131080 | tf_op jit(solution)/shard_map/dot_general | solution.py:16
  42.6 1.5 %fusion.53 = f32[128,128]{1,0:T(8,128)} fusion(bf16[128,128]{1,0:T(8,128)(2,1)S(1)} %fusion.17, bf16[3,6,128,128]{3,2,1,0:T(8,128)(2,1)} %param.18, s32[]{:T(128)S(6)} %select_n.112), kind=kOutput, calls=%fused_computation.108 | convolution fusion | flops 4194304 | bytes 131076 | tf_op jit(solution)/shard_map/dot_general | solution.py:16
  44.3 1.0 %fusion.23 = f32[128,128]{1,0:T(8,128)S(1)} fusion(bf16[128,128]{1,0:T(8,128)(2,1)S(1)} %fusion.17, bf16[3,6,128,128]{3,2,1,0:T(8,128)(2,1)} %param.18, s32[]{:T(128)S(6)} %add.217, s32[]{:T(128)S(6)} %select_n.113, bf16[384,128]{1,0:T(8,128)(2,1)S(1)} %collective-permute-done.4), kind=kOutput, calls=%fused_computation.55 | convolution fusion | flops 8404992 | bytes 163848 | tf_op jit(solution)/shard_map/dot_general | solution.py:20
  45.3 1.0 %add_convert_fusion.2 = bf16[128,128]{1,0:T(8,128)(2,1)S(1)} fusion(bf16[128,128]{1,0:T(8,128)(2,1)S(1)} %add_convert_fusion.3, bf16[384,128]{1,0:T(8,128)(2,1)S(1)} %collective-permute-done.4, f32[128,128]{1,0:T(8,128)S(1)} %fusion.23, bf16[128,128]{1,0:T(8,128)(2,1)S(1)} %fusion.18, bf16[3,6,128,128]{3,2,1,0:T(8,128)(2,1)} %param.18, s32[]{:T(128)S(6)} %add.217, ...), kind=kOutput, calls=%fused_computation.89 | convolution fusion | flops 8503296 | bytes 262152 | tf_op jit(solution)/shard_map/dot_general | solution.py:20
  46.4 1.1 %fusion.21 = bf16[128,128]{1,0:T(8,128)(2,1)S(1)} fusion(f32[128,128]{1,0:T(8,128)} %fusion.87, bf16[3,6,128,128]{3,2,1,0:T(8,128)(2,1)} %param.18, s32[]{:T(128)S(6)} %add.218, s32[]{:T(128)S(6)} %select_n.113, bf16[384,128]{1,0:T(8,128)(2,1)} %copy-done.10), kind=kOutput, calls=%fused_computation.46 | convolution fusion | flops 4227072 | bytes 163848 | tf_op jit(solution)/shard_map/dot_general | solution.py:16
  47.5 1.0 %fusion.20 = bf16[128,128]{1,0:T(8,128)(2,1)S(1)} fusion(f32[128,128]{1,0:T(8,128)} %fusion.53, bf16[3,6,128,128]{3,2,1,0:T(8,128)(2,1)} %param.18, s32[]{:T(128)S(6)} %select_n.113, bf16[384,128]{1,0:T(8,128)(2,1)} %copy-done.10), kind=kOutput, calls=%fused_computation.45 | convolution fusion | flops 4227072 | bytes 163844 | tf_op jit(solution)/shard_map/dot_general | solution.py:16
  49.2 1.4 %collective-permute-start.5 = (bf16[384,128]{1,0:T(8,128)(2,1)}, bf16[384,128]{1,0:T(8,128)(2,1)}, u32[]{:S(2)}, u32[]{:S(2)}) collective-permute-start(bf16[384,128]{1,0:T(8,128)(2,1)} %pad_maximum_fusion.5), channel_id=1, source_target_pairs={{0,16},{8,24},{16,0},{24,8},{1,17},{9,25},{17,1},{25,9},{2,18},{10... | collective-permute-start | bytes 294920 | tf_op jit(solution)/shard_map/ppermute | solution.py:12
  50.6 3.5 %collective-permute-done.5 = bf16[384,128]{1,0:T(8,128)(2,1)} collective-permute-done((bf16[384,128]{1,0:T(8,128)(2,1)}, bf16[384,128]{1,0:T(8,128)(2,1)}, u32[]{:S(2)}, u32[]{:S(2)}) %collective-permute-start.5) | collective-permute-done | bytes 98336 | tf_op jit(solution)/shard_map/ppermute | solution.py:12
  54.2 1.7 %fusion.25 = f32[128,128]{1,0:T(8,128)} fusion(bf16[128,128]{1,0:T(8,128)(2,1)} %copy-done.8, bf16[3,6,128,128]{3,2,1,0:T(8,128)(2,1)} %param.18, s32[]{:T(128)S(6)} %add.217, s32[]{:T(128)S(6)} %select_n.120, bf16[384,128]{1,0:T(8,128)(2,1)} %collective-permute-done.5), kind=kOutput, calls=%fused_computation.57 | convolution fusion | flops 8404992 | bytes 163848 | tf_op jit(solution)/shard_map/dot_general | solution.py:20
  55.8 1.8 %add_convert_fusion.1 = bf16[128,128]{1,0:T(8,128)(2,1)} fusion(bf16[128,128]{1,0:T(8,128)(2,1)S(1)} %add_convert_fusion.2, bf16[384,128]{1,0:T(8,128)(2,1)} %collective-permute-done.5, f32[128,128]{1,0:T(8,128)} %fusion.25, bf16[128,128]{1,0:T(8,128)(2,1)} %copy-done.7, bf16[3,6,128,128]{3,2,1,0:T(8,128)(2,1)} %param.18, s32[]{:T(128)S(6)} %add.217, ...), kind=kOutput, calls=%fused_computation.88 | convolution fusion | flops 8503296 | bytes 262152 | tf_op jit(solution)/shard_map/dot_general | solution.py:20
  57.6 1.2 %collective-permute-start.7 = (bf16[128,128]{1,0:T(8,128)(2,1)}, bf16[128,128]{1,0:T(8,128)(2,1)S(1)}, u32[]{:S(2)}, u32[]{:S(2)}) collective-permute-start(bf16[128,128]{1,0:T(8,128)(2,1)} %add_convert_fusion.1), channel_id=1, source_target_pairs={{0,4},{1,5},{2,6},{3,7},{4,0},{5,1},{6,2},{7,3},{8,12},{9,13},{10,... | collective-permute-start | bytes 98312 | tf_op jit(solution)/shard_map/ppermute | solution.py:12
  58.8 1.7 %fusion.24 = f32[128,128]{1,0:T(8,128)} fusion(bf16[384,128]{1,0:T(8,128)(2,1)} %collective-permute-done.5, bf16[3,6,128,128]{3,2,1,0:T(8,128)(2,1)} %param.18, s32[]{:T(128)S(6)} %add.218, s32[]{:T(128)S(6)} %select_n.112, s32[]{:T(128)S(6)} %add.217, s32[]{:T(128)S(6)} %select_n.114), kind=kOutput, calls=%fused_computation.56 | convolution fusion | flops 8404992 | bytes 163856 | tf_op jit(solution)/shard_map/dot_general | solution.py:20
  60.5 1.8 %fusion.26 = f32[128,128]{1,0:T(8,128)} fusion(f32[128,128]{1,0:T(8,128)} %fusion.24, bf16[3,6,128,128]{3,2,1,0:T(8,128)(2,1)S(1)} %copy-done, s32[]{:T(128)S(6)} %add.218, s32[]{:T(128)S(6)} %select_n.109, bf16[3,6,128,128]{3,2,1,0:T(8,128)(2,1)} %param.18, s32[]{:T(128)S(6)} %add.217, s32[]{:T(128)S(6)} %select_n.112, bf16[384,128]{1,0:T(8,128)(2,1)} %copy-done.10), kind=kOutput, calls=%fused_computation.58 | convolution fusion | flops 8421376 | bytes 229392 | tf_op jit(solution)/shard_map/dot_general | solution.py:20
  62.3 1.8 %fusion.27 = f32[128,128]{1,0:T(8,128)} fusion(f32[128,128]{1,0:T(8,128)} %fusion.26, bf16[3,6,128,128]{3,2,1,0:T(8,128)(2,1)S(1)} %copy-done, s32[]{:T(128)S(6)} %add.218, s32[]{:T(128)S(6)} %select_n.105, s32[]{:T(128)S(6)} %add.217, s32[]{:T(128)S(6)} %select_n.109, bf16[384,128]{1,0:T(8,128)(2,1)} %copy-done.11), kind=kOutput, calls=%fused_computation.59 | convolution fusion | flops 8421376 | bytes 229392 | tf_op jit(solution)/shard_map/dot_general | solution.py:20
  64.1 1.0 %fusion.14 = bf16[128,128]{1,0:T(8,128)(2,1)S(1)} fusion(f32[128,128]{1,0:T(8,128)} %fusion.27, bf16[3,6,128,128]{3,2,1,0:T(8,128)(2,1)S(1)} %copy-done, s32[]{:T(128)S(6)} %add.217, s32[]{:T(128)S(6)} %select_n.105, bf16[640,128]{1,0:T(8,128)(2,1)S(1)} %collective-permute-done.2), kind=kOutput, calls=%fused_computation.39 | convolution fusion | flops 4227072 | bytes 163848 | tf_op jit(solution)/shard_map/dot_general | solution.py:20
  65.9 2.8 %collective-permute-start.8 = (bf16[256,128]{1,0:T(8,128)(2,1)S(1)}, bf16[256,128]{1,0:T(8,128)(2,1)S(1)}, u32[]{:S(2)}, u32[]{:S(2)}) collective-permute-start(bf16[256,128]{1,0:T(8,128)(2,1)S(1)} %pad_maximum_fusion.6), channel_id=1, source_target_pairs={{0,2},{1,3},{2,0},{3,1},{4,6},{5,7},{6,4},{7,5},{8,10},{9,11},{10,... | collective-permute-start | bytes 196616 | tf_op jit(solution)/shard_map/ppermute | solution.py:12
  68.7 0.9 %fusion.38 = f32[256,128]{1,0:T(8,128)S(1)} fusion(bf16[128,128]{1,0:T(8,128)(2,1)S(1)} %get-tuple-element.12, bf16[128,128]{1,0:T(8,128)(2,1)S(1)} %get-tuple-element.11, bf16[3,1,128,128]{3,2,1,0:T(8,128)(2,1)} %param.16), kind=kOutput, calls=%fused_computation.83 | convolution fusion | flops 8519680 | bytes 229376 | tf_op jit(solution)/shard_map/dot_general | solution.py:20
  69.7 1.7 %fusion.11 = bf16[256,128]{1,0:T(8,128)(2,1)} fusion(f32[256,128]{1,0:T(8,128)S(1)} %fusion.38, bf16[3,1,128,128]{3,2,1,0:T(8,128)(2,1)} %param.16, bf16[1408,128]{1,0:T(8,128)(2,1)} %collective-permute-done), kind=kOutput, calls=%fused_computation.25 | convolution fusion | flops 8454144 | bytes 294912 | tf_op jit(solution)/shard_map/dot_general | solution.py:20
  72.2 3.8 %fusion.8 = bf16[1536,256]{1,0:T(8,128)(2,1)} fusion(s32[1536]{0:T(1024)S(1)} %reduce, bf16[1536,256]{1,0:T(8,128)(2,1)S(1)} %copy-done.4, f32[256,1536]{1,0:T(8,128)S(1)} %copy-done.2, bf16[256,128]{1,0:T(8,128)(2,1)} %fusion.11, f32[]{:T(128)} %bitcast.127, bf16[1,1536,128]{2,1,0:T(8,128)(2,1)S(1)} %copy-done.6), kind=kOutput, calls=%fused_computation.10 | convolution fusion | flops 1313341440 | bytes 3610628 | tf_op jit(solution)/shard_map/dot_general | solution.py:16
  76.1 1.0 %broadcast_select_fusion.1 = (bf16[512,128]{1,0:T(8,128)(2,1)S(1)}, bf16[512,128]{1,0:T(8,128)(2,1)S(1)}) fusion(bf16[512,128]{1,0:T(8,128)(2,1)} %collective-permute-done.9, pred[]{:T(512)S(6)} %eq.27, bf16[256,128]{1,0:T(8,128)(2,1)S(1)} %get-tuple-element.8, bf16[256,128]{1,0:T(8,128)(2,1)S(1)} %get-tuple-element.7), kind=kLoop, calls=%fused_computation.79 | loop fusion | flops 393216 | bytes 524289 | tf_op jit(solution)/shard_map/jit(_where)/select_n | solution.py:28
  (82 shorter events, 12.0 us)
Async XLA Ops:
  0.6 25.4 %copy-start = (bf16[3,6,128,128]{3,2,1,0:T(8,128)(2,1)S(1)}, bf16[3,6,128,128]{3,2,1,0:T(8,128)(2,1)}, u32[]{:S(2)}) copy-start(bf16[3,6,128,128]{3,2,1,0:T(8,128)(2,1)} %param.17) | copy-start | bytes 1769476
  0.6 2.2 %copy-start.14 = (s32[1,1536]{1,0:T(1,128)S(1)}, s32[1,1536]{1,0:T(1,128)}, u32[]{:S(2)}) copy-start(s32[1,1536]{1,0:T(1,128)} %param.12) | copy-start | bytes 18436
  0.7 2.2 %copy-start.3 = (bf16[1536,256]{1,0:T(8,128)(2,1)S(1)}, bf16[1536,256]{1,0:T(8,128)(2,1)}, u32[]{:S(2)}) copy-start(bf16[1536,256]{1,0:T(8,128)(2,1)} %param.11) | copy-start | bytes 2359300
  3.9 4.2 %copy-start.5 = (bf16[1,1536,128]{2,1,0:T(8,128)(2,1)S(1)}, bf16[1,1536,128]{2,1,0:T(8,128)(2,1)}, u32[]{:S(2)}) copy-start(bf16[1,1536,128]{2,1,0:T(8,128)(2,1)} %param.15) | copy-start | bytes 1179652
  8.1 0.9 %copy-start.9 = (bf16[3,1,128,128]{3,2,1,0:T(8,128)(2,1)S(1)}, bf16[3,1,128,128]{3,2,1,0:T(8,128)(2,1)}, u32[]{:S(2)}) copy-start(bf16[3,1,128,128]{3,2,1,0:T(8,128)(2,1)} %param.16) | copy-start | bytes 294916
  8.1 1.2 %copy-start.15 = (bf16[1,1536,128]{2,1,0:T(8,128)(2,1)S(1)}, bf16[1,1536,128]{2,1,0:T(8,128)(2,1)}, u32[]{:S(2)}) copy-start(bf16[1,1536,128]{2,1,0:T(8,128)(2,1)} %param.14) | copy-start | bytes 1179652
  9.9 5.0 %copy-start.12 = (bf16[256,128]{1,0:T(8,128)(2,1)}, bf16[256,128]{1,0:T(8,128)(2,1)S(1)}, u32[]{:S(2)}) copy-start(bf16[256,128]{1,0:T(8,128)(2,1)S(1)} %convolution_convert_fusion.6) | copy-start | bytes 196612
  10.7 8.3 %collective-permute-start = (bf16[1408,128]{1,0:T(8,128)(2,1)}, bf16[1408,128]{1,0:T(8,128)(2,1)}, u32[]{:S(2)}, u32[]{:S(2)}) collective-permute-start(bf16[1408,128]{1,0:T(8,128)(2,1)} %pad_maximum_fusion), channel_id=1, source_target_pairs={{0,1},{1,0},{2,3},{3,2},{4,5},{5,4},{6,7},{7,6},{8,9},{9,8},{10,11... | collective-permute-start | bytes 1081352 | tf_op jit(solution)/shard_map/ppermute | solution.py:12
  14.9 1.2 %copy-start.1 = (f32[256,1536]{1,0:T(8,128)}, f32[256,1536]{1,0:T(8,128)S(1)}, u32[]{:S(2)}) copy-start(f32[256,1536]{1,0:T(8,128)S(1)} %fusion.2) | copy-start | bytes 4718596
  14.9 1.8 %copy-start.4 = (bf16[1536,256]{1,0:T(8,128)(2,1)S(1)}, bf16[1536,256]{1,0:T(8,128)(2,1)}, u32[]{:S(2)}) copy-start(bf16[1536,256]{1,0:T(8,128)(2,1)} %param.10) | copy-start | bytes 2359300
  18.8 3.3 %copy-start.13 = (bf16[256,128]{1,0:T(8,128)(2,1)S(1)}, bf16[256,128]{1,0:T(8,128)(2,1)}, u32[]{:S(2)}) copy-start(bf16[256,128]{1,0:T(8,128)(2,1)} %copy-done.12) | copy-start | bytes 196612
  18.8 2.0 %collective-permute-start.1 = (bf16[512,128]{1,0:T(8,128)(2,1)S(1)}, bf16[512,128]{1,0:T(8,128)(2,1)S(1)}, u32[]{:S(2)}, u32[]{:S(2)}) collective-permute-start(bf16[512,128]{1,0:T(8,128)(2,1)S(1)} %dynamic-slice_convert_fusion), channel_id=1, source_target_pairs={{0,1},{1,0},{2,3},{3,2},{4,5},{5,4},{6,7},{7,6},{8,9},{9,8},{10,11... | collective-permute-start | bytes 393224 | tf_op jit(solution)/shard_map/ppermute | solution.py:12
  22.9 7.5 %collective-permute-start.2 = (bf16[640,128]{1,0:T(8,128)(2,1)S(1)}, bf16[640,128]{1,0:T(8,128)(2,1)S(1)}, u32[]{:S(2)}, u32[]{:S(2)}) collective-permute-start(bf16[640,128]{1,0:T(8,128)(2,1)S(1)} %pad_maximum_fusion.1), channel_id=1, source_target_pairs={{0,2},{1,3},{2,0},{3,1},{4,6},{5,7},{6,4},{7,5},{8,10},{9,11},{10,... | collective-permute-start | bytes 491528 | tf_op jit(solution)/shard_map/ppermute | solution.py:12
  31.5 7.2 %collective-permute-start.3 = (bf16[384,128]{1,0:T(8,128)(2,1)S(1)}, bf16[384,128]{1,0:T(8,128)(2,1)S(1)}, u32[]{:S(2)}, u32[]{:S(2)}) collective-permute-start(bf16[384,128]{1,0:T(8,128)(2,1)S(1)} %pad_maximum_fusion.3), channel_id=1, source_target_pairs={{0,4},{1,5},{2,6},{3,7},{4,0},{5,1},{6,2},{7,3},{8,12},{9,13},{10,... | collective-permute-start | bytes 294920 | tf_op jit(solution)/shard_map/ppermute | solution.py:12
  38.7 0.8 %copy-start.11 = (bf16[384,128]{1,0:T(8,128)(2,1)}, bf16[384,128]{1,0:T(8,128)(2,1)S(1)}, u32[]{:S(2)}) copy-start(bf16[384,128]{1,0:T(8,128)(2,1)S(1)} %collective-permute-done.3) | copy-start | bytes 294916
  39.6 4.7 %collective-permute-start.4 = (bf16[384,128]{1,0:T(8,128)(2,1)S(1)}, bf16[384,128]{1,0:T(8,128)(2,1)S(1)}, u32[]{:S(2)}, u32[]{:S(2)}) collective-permute-start(bf16[384,128]{1,0:T(8,128)(2,1)S(1)} %pad_maximum_fusion.4), channel_id=1, source_target_pairs={{0,8},{8,0},{16,24},{24,16},{1,9},{9,1},{17,25},{25,17},{2,10},{10... | collective-permute-start | bytes 294920 | tf_op jit(solution)/shard_map/ppermute | solution.py:12
  44.3 1.0 %copy-start.10 = (bf16[384,128]{1,0:T(8,128)(2,1)}, bf16[384,128]{1,0:T(8,128)(2,1)S(1)}, u32[]{:S(2)}) copy-start(bf16[384,128]{1,0:T(8,128)(2,1)S(1)} %collective-permute-done.4) | copy-start | bytes 294916
  46.3 25.9 %copy-start.2 = (f32[256,1536]{1,0:T(8,128)S(1)}, f32[256,1536]{1,0:T(8,128)}, u32[]{:S(2)}) copy-start(f32[256,1536]{1,0:T(8,128)} %copy-done.1) | copy-start | bytes 4718596
  46.3 25.9 %copy-start.6 = (bf16[1,1536,128]{2,1,0:T(8,128)(2,1)S(1)}, bf16[1,1536,128]{2,1,0:T(8,128)(2,1)}, u32[]{:S(2)}) copy-start(bf16[1,1536,128]{2,1,0:T(8,128)(2,1)} %param.15) | copy-start | bytes 1179652
  47.5 1.0 %copy-start.7 = (bf16[128,128]{1,0:T(8,128)(2,1)}, bf16[128,128]{1,0:T(8,128)(2,1)S(1)}, u32[]{:S(2)}) copy-start(bf16[128,128]{1,0:T(8,128)(2,1)S(1)} %fusion.21) | copy-start | bytes 98308
  48.6 0.7 copy-start.8
  49.2 4.9 %collective-permute-start.5 = (bf16[384,128]{1,0:T(8,128)(2,1)}, bf16[384,128]{1,0:T(8,128)(2,1)}, u32[]{:S(2)}, u32[]{:S(2)}) collective-permute-start(bf16[384,128]{1,0:T(8,128)(2,1)} %pad_maximum_fusion.5), channel_id=1, source_target_pairs={{0,16},{8,24},{16,0},{24,8},{1,17},{9,25},{17,1},{25,9},{2,18},{10... | collective-permute-start | bytes 294920 | tf_op jit(solution)/shard_map/ppermute | solution.py:12
  57.6 7.5 %collective-permute-start.7 = (bf16[128,128]{1,0:T(8,128)(2,1)}, bf16[128,128]{1,0:T(8,128)(2,1)S(1)}, u32[]{:S(2)}, u32[]{:S(2)}) collective-permute-start(bf16[128,128]{1,0:T(8,128)(2,1)} %add_convert_fusion.1), channel_id=1, source_target_pairs={{0,4},{1,5},{2,6},{3,7},{4,0},{5,1},{6,2},{7,3},{8,12},{9,13},{10,... | collective-permute-start | bytes 98312 | tf_op jit(solution)/shard_map/ppermute | solution.py:12
  65.1 3.7 %collective-permute-start.6 = (bf16[128,128]{1,0:T(8,128)(2,1)S(1)}, bf16[128,128]{1,0:T(8,128)(2,1)S(1)}, u32[]{:S(2)}, u32[]{:S(2)}) collective-permute-start(bf16[128,128]{1,0:T(8,128)(2,1)S(1)} %fusion.14), channel_id=1, source_target_pairs={{0,1},{1,0},{2,3},{3,2},{4,5},{5,4},{6,7},{7,6},{8,9},{9,8},{10,11... | collective-permute-start | bytes 98312 | tf_op jit(solution)/shard_map/ppermute | solution.py:12
  65.9 5.5 %collective-permute-start.8 = (bf16[256,128]{1,0:T(8,128)(2,1)S(1)}, bf16[256,128]{1,0:T(8,128)(2,1)S(1)}, u32[]{:S(2)}, u32[]{:S(2)}) collective-permute-start(bf16[256,128]{1,0:T(8,128)(2,1)S(1)} %pad_maximum_fusion.6), channel_id=1, source_target_pairs={{0,2},{1,3},{2,0},{3,1},{4,6},{5,7},{6,4},{7,5},{8,10},{9,11},{10,... | collective-permute-start | bytes 196616 | tf_op jit(solution)/shard_map/ppermute | solution.py:12
  72.2 3.9 %collective-permute-start.9 = (bf16[512,128]{1,0:T(8,128)(2,1)}, bf16[512,128]{1,0:T(8,128)(2,1)}, u32[]{:S(2)}, u32[]{:S(2)}) collective-permute-start(bf16[512,128]{1,0:T(8,128)(2,1)} %pad_maximum_fusion.2), channel_id=1, source_target_pairs={{0,1},{1,0},{2,3},{3,2},{4,5},{5,4},{6,7},{7,6},{8,9},{9,8},{10,11... | collective-permute-start | bytes 393224 | tf_op jit(solution)/shard_map/ppermute | solution.py:12

commit v2 on v0

v2 whole, which is shorter than its diff:
```python
import functools

import jax
import jax.numpy as jnp
from jax import lax
from jax.experimental import pallas as pl
from jax.experimental.pallas import tpu as pltpu
from jax.sharding import PartitionSpec as P

BF = jnp.bfloat16
F32 = jnp.float32
I16 = jnp.int16
MIB = 2**20
VM = pl.BlockSpec(memory_space=pltpu.VMEM)
SM = pl.BlockSpec(memory_space=pltpu.SMEM)
FAR = pl.BlockSpec(memory_space=pltpu.HBM)


def mm(a, b):
    return lax.dot_general(a, b, (((1,), (0,)), ((), ())), preferred_element_type=F32)


def mmt(a, b):
    return lax.dot_general(a, b, (((1,), (1,)), ((), ())), preferred_element_type=F32)


def shape(dims, kind=BF):
    return jax.ShapeDtypeStruct(dims, kind)


def cost(flops, moved):
    return pl.CostEstimate(flops=flops, bytes_accessed=moved, transcendentals=0)


def swap(block, axis, mask):
    count = lax.axis_size(axis)
    return lax.ppermute(block, axis, [(i, i ^ mask) for i in range(count)])


class Phase:
    def __init__(self, axis, first, bits, height, sizes):
        self.axis, self.first, self.bits, self.height = axis, first, bits, height
        self.parts = 1 << bits
        self.scatter = axis == "leaf"
        self.leaves, self.groups = sizes

    def index(self):
        return lax.axis_index(self.axis)

    def place(self):
        return (self.index() >> self.first) & (self.parts - 1)

    def node(self, level, j):
        bit = self.first + level
        if self.axis == "leaf":
            start = sum(self.leaves >> s for s in range(1, bit))
        else:
            start = sum(self.groups >> s for s in range(bit))
        return start + ((self.index() >> (self.first + self.bits)) << (self.bits - level)) + j


def plan(leaves, groups):
    phases = []
    leaf_levels, group_levels = leaves.bit_length() - 1, groups.bit_length() - 1
    for axis, low, high in (("leaf", 1, leaf_levels), ("grp", 0, group_levels)):
        bit = low
        while bit < high:
            bits = min(2, high - bit)
            height = bit if axis == "leaf" else leaf_levels + bit
            phases.append(Phase(axis, bit, bits, height, (leaves, groups)))
            bit += bits
    return phases


def front_kernel(chunk, ridge_ref, order_far, ops_far, d_far, r_far, diag_far, up_far, down_far,
                 msg_ref, keep_ref, gown_ref, dense_far,
                 order_v, ops_v, d_v, r_v, diag_v, up_v, down_v, bt, xt, dense_v, sems):
    points, nrhs = d_v.shape
    half = nrhs // 2
    n = points // chunk
    flip = (lax.axis_index("leaf") & 1) == 0

    def start(src, dst, i):
        copy = pltpu.make_async_copy(src, dst, sems.at[i])
        copy.start()
        return copy

    c_order = start(order_far, order_v, 0)
    c_d = start(d_far, d_v, 1)
    c_r = start(r_far, r_v, 2)
    c_up = start(up_far.at[0], up_v, 3)
    c_down = start(down_far.at[0], down_v, 4)
    c_ops = start(ops_far, ops_v, 5)
    c_order.wait()
    c_d.wait()
    c_diag = [
        start(diag_far.at[0, pl.ds(i * chunk, chunk)], diag_v.at[pl.ds(i * chunk, chunk)], 6 + i)
        for i in range(n)
    ]
    bt[:nrhs] = d_v[...].T
    c_r.wait()
    bt[nrhs:] = r_v[...].T
    rows = lax.broadcasted_iota(jnp.int32, (points, chunk), 0).astype(I16)

    def spread(i, carry):
        at = pl.ds(pl.multiple_of(i * chunk, chunk), chunk)
        hot = jnp.where(rows == order_v[:, at].astype(I16), BF(1), BF(0))
        xt[:, at] = mm(bt[...], hot).astype(BF)
        return carry

    lax.fori_loop(0, n, spread, 0)
    c_up.wait()
    c_down.wait()
    c_ops.wait()
    st = mm(xt[:nrhs], up_v[...]).astype(BF)
    vt = mm(xt[...], down_v[...]).astype(BF)
    lift = mm(st, ops_v[0, 0]).astype(BF)
    vr = mm(vt, ops_v[1, 0]).astype(BF)
    vb = mm(vt, ops_v[2, 0]).astype(BF)
    b = nrhs + half
    msg_ref[:nrhs] = st
    msg_ref[nrhs:b] = jnp.where(flip, lift[half:], lift[:half])
    msg_ref[b : b + 2 * nrhs] = vr
    msg_ref[b + 2 * nrhs : b + 4 * nrhs] = vb
    keep_ref[:half] = jnp.where(flip, st[:half], st[half:])
    keep_ref[half:nrhs] = jnp.where(flip, lift[:half], lift[half:])
    keep_ref[nrhs : 3 * nrhs] = vr
    keep_ref[3 * nrhs :] = vb
    c_out = []
    for i in range(n):
        c_diag[i].wait()
        at = pl.ds(i * chunk, chunk)
        dense_v[at] = mmt(diag_v[at], xt[:nrhs]).astype(BF)
        c_out.append(start(dense_v.at[at], dense_far.at[at], 6 + n + i))
    gram = mm(xt[...], dense_v[...]) + ridge_ref[0] * mm(bt[...], d_v[...])
    msg_ref[b + 4 * nrhs :] = jnp.where(flip, gram[:, half:], gram[:, :half]).astype(BF)
    gown_ref[...] = jnp.where(flip, gram[:, :half], gram[:, half:])
    for copy in c_out:
        copy.wait()


def front(ridge, order, ops, d, r, diag, up, down):
    points, nrhs = d.shape
    rank = up.shape[2]
    half = nrhs // 2
    chunk = points // 2 if points // 2 % 128 == 0 else points
    n = points // chunk
    return pl.pallas_call(
        functools.partial(front_kernel, chunk),
        out_shape=(
            shape((7 * nrhs + half, rank)),
            shape((5 * nrhs, rank)),
            shape((2 * nrhs, half), F32),
            shape((points, nrhs)),
        ),
        in_specs=[SM] + [FAR] * 7,
        out_specs=(VM, VM, VM, FAR),
        scratch_shapes=[
            pltpu.VMEM(order.shape, jnp.int32),
            pltpu.VMEM(ops.shape, BF),
            pltpu.VMEM((points, nrhs), BF),
            pltpu.VMEM((points, nrhs), BF),
            pltpu.VMEM((points, points), BF),
            pltpu.VMEM((points, rank), BF),
            pltpu.VMEM((points, rank), BF),
            pltpu.VMEM((2 * nrhs, points), BF),
            pltpu.VMEM((2 * nrhs, points), BF),
            pltpu.VMEM((points, nrhs), BF),
            pltpu.SemaphoreType.DMA((6 + 2 * n,)),
        ],
        compiler_params=pltpu.CompilerParams(vmem_limit_bytes=FRONT_LIMIT),
        cost_estimate=cost(5 * points * points * nrhs, 2 * points * points),
        name="front",
    )(ridge, order, ops, d, r, diag, up, down)


FRONT_LIMIT = 61 * MIB


def emit(phase, s, v, g, v_s, g_s, outs):
    if phase is None:
        outs[0][...] = g.astype(BF)
        return
    rank = s.shape[0]
    if not phase.scatter:
        rows = v.shape[0]
        outs[0][:rank] = s
        outs[0][rank : rank + rows] = v
        outs[0][rank + rows :] = g.astype(BF)
        return
    v_s[...] = v
    g_s[...] = g
    piece = v.shape[0] // phase.parts
    place = phase.place()
    for mask in range(1, phase.parts):
        at = pl.ds(pl.multiple_of((place ^ mask) * piece, piece), piece)
        outs[mask][:rank] = s
        outs[mask][rank : rank + piece] = v_s[at]
        outs[mask][rank + piece :] = g_s[at].astype(BF)
    at = pl.ds(pl.multiple_of(place * piece, piece), piece)
    outs[0][:rank] = s
    outs[0][rank:] = v_s[at]
    outs[-1][...] = g_s[at]


def emit_shapes(phase, cols, rows, rank):
    if phase is None:
        return [shape((rows, cols))]
    if not phase.scatter:
        return [shape((cols + 2 * rows, rank))]
    piece = rows // phase.parts
    return (
        [shape((cols + piece, rank))]
        + [shape((cols + 2 * piece, rank))] * (phase.parts - 1)
        + [shape((piece, cols), F32)]
    )


def core_kernel(phase, got, keep, gown, *rest):
    outs, (v_s, g_s) = rest[:-2], rest[-2:]
    half = gown.shape[1]
    nrhs = 2 * half
    flip = (lax.axis_index("leaf") & 1) == 0
    b = nrhs + half
    sib = jnp.where(flip, got[:half], got[half:nrhs])
    s = (keep[half:nrhs].astype(F32) + got[nrhs:b].astype(F32)).astype(BF)
    v = (keep[nrhs : 3 * nrhs].astype(F32) + got[b : b + 2 * nrhs].astype(F32)).astype(BF)
    g = (
        gown[...]
        + got[b + 4 * nrhs :].astype(F32)
        + (mmt(keep[3 * nrhs :], sib) + mmt(got[b + 2 * nrhs : b + 4 * nrhs], keep[:half]))
    )
    emit(phase, s, v, g, v_s, g_s, outs)


def core_merge(phase, got, keep, gown):
    rows, cols = gown.shape
    rank = keep.shape[1]
    return pl.pallas_call(
        functools.partial(core_kernel, phase),
        out_shape=tuple(emit_shapes(phase, cols, rows, rank)),
        in_specs=[VM] * 3,
        out_specs=tuple([VM] * len(emit_shapes(phase, cols, rows, rank))),
        scratch_shapes=[pltpu.VMEM((rows, rank), BF), pltpu.VMEM((rows, cols), F32)],
        compiler_params=pltpu.CompilerParams(vmem_limit_bytes=8 * MIB),
        cost_estimate=cost(4 * rows * cols * rank, 4 * rows * rank),
        name="core_merge",
    )(got, keep, gown)


def merge_kernel(phase, following, last, own, gots, gown, ops, outs, scratch):
    v_s, g_s, s_in, v_in, g_in, levels = scratch
    cols, rank = s_in.shape[1:]
    rows = v_in.shape[1]
    place = phase.place()
    blocks = [(place, own)] + [(place ^ (m + 1), got) for m, got in enumerate(gots)]
    for slot, block in blocks:
        s_in[slot] = block[:cols]
        v_in[slot] = block[cols : cols + rows]
        if not phase.scatter:
            g_in[slot] = block[cols + rows :]
    if phase.scatter:
        g = gown[...]
        for got in gots:
            g = g + got[cols + rows :].astype(F32)
    else:
        g = g_in[0].astype(F32)
        for j in range(1, phase.parts):
            g = g + g_in[j].astype(F32)
    s = [s_in[j] for j in range(phase.parts)]
    v = [v_in[j] for j in range(phase.parts)]
    sib_out = outs[-1]
    for level in range(phase.bits):
        for j, block in enumerate(s):
            levels[j] = block
        sib_out[level] = levels[(place >> level) ^ 1]
        at = [phase.node(level, j) for j in range(len(s))]
        up_s, up_v = [], []
        for a in range(0, len(s), 2):
            c = a + 1
            va = mm(v[a], ops[2, at[a]]).astype(BF)
            vc = mm(v[c], ops[2, at[c]]).astype(BF)
            g = g + (mmt(va, s[c]) + mmt(vc, s[a]))
            if not (last and level == phase.bits - 1):
                up_s.append((mm(s[a], ops[0, at[a]]) + mm(s[c], ops[0, at[c]])).astype(BF))
                up_v.append((mm(v[a], ops[1, at[a]]) + mm(v[c], ops[1, at[c]])).astype(BF))
        s, v = up_s, up_v
    emit(following, s[0] if s else None, v[0] if v else None, g, v_s, g_s, outs[:-1])


def merge(phase, following, own, gots, gown, ops, cols):
    rank = own.shape[1]
    rows = gots[0].shape[0] // 2 - cols // 2
    outs = emit_shapes(following, cols, rows, rank) + [shape((phase.bits, cols, rank))]
    args = [own, *gots] + ([gown] if phase.scatter else []) + [ops]

    def kernel(*refs):
        ins, rest = refs[: len(args)], refs[len(args) :]
        merge_kernel(
            phase,
            following,
            following is None,
            ins[0],
            ins[1 : phase.parts],
            ins[phase.parts] if phase.scatter else None,
            ins[-1],
            rest[: len(outs)],
            rest[len(outs) :],
        )

    return pl.pallas_call(
        kernel,
        out_shape=tuple(outs),
        in_specs=[VM] * len(args),
        out_specs=tuple([VM] * len(outs)),
        scratch_shapes=[
            pltpu.VMEM((rows, rank), BF),
            pltpu.VMEM((rows, cols), F32),
            pltpu.VMEM((phase.parts, cols, rank), BF),
            pltpu.VMEM((phase.parts, rows, rank), BF),
            pltpu.VMEM((phase.parts, rows, cols), BF),
            pltpu.VMEM((phase.parts, cols, rank), BF),
        ],
        compiler_params=pltpu.CompilerParams(vmem_limit_bytes=8 * MIB),
        cost_estimate=cost(40 * rows * cols * rank, 20 * rows * rank),
        name=f"merge_{phase.axis}{phase.first}",
    )(*args)


def down_kernel(phases, *refs):
    sibs, (inner, top, out) = refs[: len(phases)], refs[len(phases) :]
    coarse = None
    for phase, sib in reversed(list(zip(phases, sibs))):
        ops = inner if phase.axis == "leaf" else top
        for level in reversed(range(phase.bits)):
            at = phase.node(level, phase.place() >> level)
            term = mmt(sib[level], ops[2, at])
            if coarse is not None:
                term = term + mmt(coarse, ops[1, at])
            coarse = term.astype(BF)
    out[...] = coarse


def down_pass(phases, sibs, inner, top):
    cols, rank = sibs[0].shape[1:]
    return pl.pallas_call(
        functools.partial(down_kernel, phases),
        out_shape=shape((cols, rank)),
        in_specs=[VM] * (len(sibs) + 2),
        out_specs=VM,
        compiler_params=pltpu.CompilerParams(vmem_limit_bytes=8 * MIB),
        cost_estimate=cost(20 * cols * rank * rank, 20 * cols * rank),
        name="down_pass",
    )(*sibs, inner, top)


def image_kernel(chunk, ridge_ref, order, own, other, got, ops, down, dense, d, out, local):
    points, nrhs = d.shape
    half = own.shape[0]
    flip = (lax.axis_index("leaf") & 1) == 0
    low = jnp.where(flip, own[...], other[...])
    high = jnp.where(flip, other[...], own[...])
    parent = jnp.concatenate([low, high], 0)
    coarse = (mmt(got[:nrhs], ops[2, 0]) + mmt(parent, ops[1, 0])).astype(BF)
    local[...] = (dense[...].astype(F32) + mmt(down[0], coarse)).astype(BF)
    to = order[...].astype(I16)

    def place(i, carry):
        at = pl.ds(pl.multiple_of(i * chunk, chunk), chunk)
        rows = (lax.broadcasted_iota(jnp.int32, (chunk, points), 0) + i * chunk).astype(I16)
        hot = jnp.where(rows == to, BF(1), BF(0))
        out[at] = (mm(hot, local[...]) + ridge_ref[0] * d[at].astype(F32)).astype(BF)
        return carry

    lax.fori_loop(0, points // chunk, place, 0)


def image_of(ridge, order, own, other, got, ops, down, dense, d):
    points, nrhs = d.shape
    chunk = points // 3 if points % 384 == 0 else points
    return pl.pallas_call(
        functools.partial(image_kernel, chunk),
        out_shape=shape((points, nrhs)),
        in_specs=[SM] + [VM] * 8,
        out_specs=VM,
        scratch_shapes=[pltpu.VMEM((points, nrhs), BF)],
        compiler_params=pltpu.CompilerParams(vmem_limit_bytes=24 * MIB),
        cost_estimate=cost(2 * points * points * nrhs, 6 * points * nrhs),
        name="image",
    )(ridge, order, own, other, got, ops, down, dense, d)


def join_kernel(phase, *refs):
    out = refs[-1]
    rows = refs[0].shape[0]
    place = phase.place()
    for mask in range(phase.parts):
        out[pl.ds(pl.multiple_of((place ^ mask) * rows, rows), rows)] = refs[mask][...]


def join(phase, pieces):
    rows, cols = pieces[0].shape
    return pl.pallas_call(
        functools.partial(join_kernel, phase),
        out_shape=shape((rows * phase.parts, cols)),
        in_specs=[VM] * phase.parts,
        out_specs=VM,
        compiler_params=pltpu.CompilerParams(vmem_limit_bytes=4 * MIB),
        name="join",
    )(*pieces)


def finish_kernel(total, own, other, first, second):
    half = own.shape[1]
    nrhs = 2 * half
    flip = (lax.axis_index("leaf") & 1) == 0
    low = jnp.where(flip, own[...], other[...]).astype(F32) / total
    high = jnp.where(flip, other[...], own[...]).astype(F32) / total
    first[:, :half] = low[:nrhs]
    first[:, half:] = high[:nrhs]
    second[:, :half] = low[nrhs:]
    second[:, half:] = high[nrhs:]


def finish(total, own, other):
    rows, half = own.shape
    return pl.pallas_call(
        functools.partial(finish_kernel, total),
        out_shape=(shape((rows // 2, 2 * half), F32), shape((rows // 2, 2 * half), F32)),
        in_specs=[VM] * 2,
        out_specs=(VM, VM),
        compiler_params=pltpu.CompilerParams(vmem_limit_bytes=4 * MIB),
        name="finish",
    )(own, other)


def body(
    direction,
    residual,
    leaf_order,
    diag_block,
    up_basis,
    down_basis,
    leaf_ops,
    inner_ops,
    top_ops,
    ridge_shift,
):
    leaves, groups = lax.axis_size("leaf"), lax.axis_size("grp")
    phases = plan(leaves, groups)
    points, nrhs = direction.shape
    half = nrhs // 2
    message, keep, gown, dense = front(
        ridge_shift, leaf_order, leaf_ops, direction, residual, diag_block, up_basis, down_basis
    )
    got0 = swap(message, "leaf", 1)
    sent = core_merge(phases[0], got0, keep, gown)
    sibs = []
    for i, phase in enumerate(phases):
        following = phases[i + 1] if i + 1 < len(phases) else None
        masks = range(1, phase.parts)
        out = [sent[m] if phase.scatter else sent[0] for m in masks]
        gots = [swap(out[m - 1], phase.axis, m << phase.first) for m in masks]
        *sent, sib = merge(
            phase,
            following,
            sent[0],
            gots,
            sent[-1] if phase.scatter else None,
            inner_ops if phase.axis == "leaf" else top_ops,
            half,
        )
        sibs.append(sib)
    piece = sent[0]
    coarse = down_pass(phases, sibs, inner_ops, top_ops)
    coarse_other = swap(coarse, "leaf", 1)
    image = image_of(
        ridge_shift, leaf_order, coarse, coarse_other, got0, leaf_ops, down_basis, dense, direction
    )
    for phase in reversed(phases):
        if phase.scatter:
            gots = [swap(piece, "leaf", m << phase.first) for m in range(1, phase.parts)]
            piece = join(phase, [piece, *gots])
    other = swap(piece, "leaf", 1)
    curvature, correlation = finish(points * leaves * groups, piece, other)
    return image, curvature, correlation


def solution(mesh):
    return jax.shard_map(
        body,
        mesh=mesh,
        in_specs=(
            P(("grp", "leaf"), None),
            P(("grp", "leaf"), None),
            P(("grp", "leaf"), None),
            P(("grp", "leaf"), None, None),
            P(("grp", "leaf"), None, None),
            P(("grp", "leaf"), None, None),
            P(None, ("grp", "leaf"), None, None),
            P(None, "grp", None, None),
            P(),
            P(),
        ),
        out_specs=(P(("grp", "leaf"), None), P(), P()),
        check_vma=False,
    )
```

time: 203 us -> 52.2 us (0.26)
  waiting for transfers between devices: 134 us -> 16.5 us
  matrix products: 18.4 us -> 0 us
  Pallas kernels: 0 us -> 16.6 us
  between operations: 14.9 us -> 1.45 us
  local copies, waits for them, and re-layouts: 16.2 us -> 3.08 us
  other arithmetic: 2.88 us -> 0 us
    psum x1 -> x0, waiting for transfers between devices: 126 us -> none  [body(): lax.psum((curvature_part, correlation_part), ('grp', 'leaf'))]
    dot_general x14 -> x0, matrix products: 18.4 us -> none  [the longest x5 5.26 us: body(): passed = jnp.dot(operators[1], coarse, preferred_element_type=jnp.float32)]
    pallas_call x0 -> x8, Pallas kernels: none -> 16.6 us  [the longest x1 10.4 us: front(): pl.pallas_call(functools.partial(front_kernel, chunk), out_shape=(shape((...]
    ppermute x9 -> x12, waiting for transfers between devices: 8.29 us -> 16.5 us  [swap(): return lax.ppermute(block, axis, [(i, i ^ mask) for i in range(count)])]
    scatter x1 -> x0, local copies, waits for them, and re-layouts: 7.8 us -> none  [body(): restored = jnp.zeros(local.shape, jnp.float32).at[ordering].set(local)]
    gather x1 -> x0, local copies, waits for them, and re-layouts: 4.93 us -> none  [body(): ordered = jnp.take(direction, ordering, axis=0)]
    ppermute x9 -> x12, starting transfers between devices: 15.1 us -> 14.3 us  [swap(): return lax.ppermute(block, axis, [(i, i ^ mask) for i in range(count)])]
  transfers between devices with their start and end apart: 10 -> 12, of which waited for: 5 -> 8; matrix products, arithmetic and copies ran while one was open for 6% -> 0% of each run, Pallas kernels for 0% -> 7%
where the time goes in v2:
time: 52.2 us; the launch traced here: 52 us
  Pallas kernels  16.6 us (32%)
  waiting for transfers between devices  16.5 us (32%)
  starting transfers between devices  14.3 us (27%)
  local copies, waits for them, and re-layouts  3.08 us (6%)
  between operations  1.45 us (3%)
    ppermute x12, waiting for transfers between devices, swap(): return lax.ppermute(block, axis, [(i, i ^ mask) for i in range(count)])  16.5 us
    ppermute x12, starting transfers between devices, swap(): return lax.ppermute(block, axis, [(i, i ^ mask) for i in range(count)])  14.3 us
    pallas_call x1, Pallas kernels, front(): pl.pallas_call(functools.partial(front_kernel, chunk), out_shape=(shape((...  10.4 us
    pallas_call x1, Pallas kernels, image_of(): pl.pallas_call(functools.partial(image_kernel, chunk), out_shape=shape((p...  3.22 us
    unnamed x18, local copies, waits for them, and re-layouts  3.08 us
    pallas_call x2, Pallas kernels, merge(): pl.pallas_call(kernel, out_shape=tuple(outs), in_specs=[VM] * len(args),...  1.32 us
  transfers between devices with their start and end apart: 12, of which 8 were waited for; matrix products, arithmetic and copies ran while one was open for 0% of the time, Pallas kernels for 7%

profile of v2, /device:TPU:0, one launch (start us, length us, event | category | flops | bytes accessed | tf_op | source)
XLA Modules:
  0.0 52.0 jit_solution(12027225693049667573)
XLA Ops:
  1.3 10.4 %front.1 = (bf16[1920,128]{1,0:T(8,128)(2,1)}, bf16[1280,128]{1,0:T(8,128)(2,1)}, f32[512,128]{1,0:T(8,128)}, bf16[1536,256]{1,0:T(8,128)(2,1)}) custom-call(f32[1]{0:T(128)S(6)} %copy.13.ridge_ref, s32[1,1536]{1,0:T(1,128)} %order.1, bf16[3,1,128,128]{3,2,1,0:T(8,128)(2,1)} %ops.1, bf16[1536,256]{1,0:T(8,128)(2,1)} %d.1, bf16[1536,256]{1,0:T(8,128)(2,1)} %r_far.1, ...), custom_call_target="tpu_custom_call" | custom-call | flops 3019898880 | bytes 4718592 | tf_op jit(solution)/shard_map/front/pallas_call | solution.py:148
  11.7 0.6 %collective-permute-start = (bf16[1920,128]{1,0:T(8,128)(2,1)}, bf16[1920,128]{1,0:T(8,128)(2,1)S(1)}, u32[]{:S(2)}, u32[]{:S(2)}) collective-permute-start(bf16[1920,128]{1,0:T(8,128)(2,1)} %get-tuple-element.18), channel_id=1, source_target_pairs={{0,1},{1,0},{2,3},{3,2},{4,5},{5,4},{6,7},{7,6},{8,9},{9,8},{10,11... | collective-permute-start | bytes 1474568 | tf_op jit(solution)/shard_map/ppermute | solution.py:37
  12.3 1.7 %collective-permute-done.got = bf16[1920,128]{1,0:T(8,128)(2,1)S(1)} collective-permute-done((bf16[1920,128]{1,0:T(8,128)(2,1)}, bf16[1920,128]{1,0:T(8,128)(2,1)S(1)}, u32[]{:S(2)}, u32[]{:S(2)}) %collective-permute-start) | collective-permute-done | bytes 491552 | tf_op jit(solution)/shard_map/ppermute | solution.py:37
  14.0 1.0 %copy-done.2 = bf16[1280,128]{1,0:T(8,128)(2,1)S(1)} copy-done((bf16[1280,128]{1,0:T(8,128)(2,1)S(1)}, bf16[1280,128]{1,0:T(8,128)(2,1)}, u32[]{:S(2)}) %copy-start.2) | copy-done | bytes 327704
  14.9 0.9 %copy-done.3 = f32[512,128]{1,0:T(8,128)S(1)} copy-done((f32[512,128]{1,0:T(8,128)S(1)}, f32[512,128]{1,0:T(8,128)}, u32[]{:S(2)}) %copy-start.3) | copy-done | bytes 262168
  15.9 0.3 core_merge.1
  16.2 3.0 %collective-permute-start.1 = (bf16[384,128]{1,0:T(8,128)(2,1)S(1)}, bf16[384,128]{1,0:T(8,128)(2,1)S(1)}, u32[]{:S(2)}, u32[]{:S(2)}) collective-permute-start(bf16[384,128]{1,0:T(8,128)(2,1)S(1)} %get-tuple-element.22), channel_id=1, source_target_pairs={{0,2},{1,3},{2,0},{3,1},{4,6},{5,7},{6,4},{7,5},{8,10},{9,11},{10,... | collective-permute-start | bytes 294920 | tf_op jit(solution)/shard_map/ppermute | solution.py:37
  19.2 2.6 %collective-permute-start.2 = (bf16[384,128]{1,0:T(8,128)(2,1)S(1)}, bf16[384,128]{1,0:T(8,128)(2,1)S(1)}, u32[]{:S(2)}, u32[]{:S(2)}) collective-permute-start(bf16[384,128]{1,0:T(8,128)(2,1)S(1)} %get-tuple-element.23), channel_id=1, source_target_pairs={{0,4},{1,5},{2,6},{3,7},{4,0},{5,1},{6,2},{7,3},{8,12},{9,13},{10,... | collective-permute-start | bytes 294920 | tf_op jit(solution)/shard_map/ppermute | solution.py:37
  21.8 0.0 collective-permute-start.3
  21.8 0.5 collective-permute-done.1.refs_1_
  22.3 7.6 %collective-permute-done.2.refs_2_ = bf16[384,128]{1,0:T(8,128)(2,1)S(1)} collective-permute-done((bf16[384,128]{1,0:T(8,128)(2,1)S(1)}, bf16[384,128]{1,0:T(8,128)(2,1)S(1)}, u32[]{:S(2)}, u32[]{:S(2)}) %collective-permute-start.2) | collective-permute-done | bytes 98336 | tf_op jit(solution)/shard_map/ppermute | solution.py:37
  29.9 0.0 collective-permute-done.3.refs_3_
  29.9 0.6 %merge_leaf1.1 = (bf16[384,128]{1,0:T(8,128)(2,1)S(1)}, bf16[2,128,128]{2,1,0:T(8,128)(2,1)S(1)}) custom-call(bf16[256,128]{1,0:T(8,128)(2,1)S(1)} %get-tuple-element.21.refs_0_, bf16[384,128]{1,0:T(8,128)(2,1)S(1)} %collective-permute-done.1.refs_1_, bf16[384,128]{1,0:T(8,128)(2,1)S(1)} %collective-permute-done.2.refs_2_, ...), custom_call_target="tpu_custom_call" | custom-call | flops 83886080 | bytes 327680 | tf_op jit(solution)/shard_map/merge_leaf1/pallas_call | solution.py:311
  30.5 2.5 %collective-permute-start.6 = (bf16[384,128]{1,0:T(8,128)(2,1)S(1)}, bf16[384,128]{1,0:T(8,128)(2,1)S(1)}, u32[]{:S(2)}, u32[]{:S(2)}) collective-permute-start(bf16[384,128]{1,0:T(8,128)(2,1)S(1)} %get-tuple-element.27.refs_0_), channel_id=1, source_target_pairs={{0,24},{8,16},{16,8},{24,0},{1,25},{9,17},{17,9},{25,1},{2,26},{10... | collective-permute-start | bytes 294920 | tf_op jit(solution)/shard_map/ppermute | solution.py:37
  33.0 0.5 collective-permute-start.5
  33.5 0.6 %collective-permute-start.4 = (bf16[384,128]{1,0:T(8,128)(2,1)S(1)}, bf16[384,128]{1,0:T(8,128)(2,1)S(1)}, u32[]{:S(2)}, u32[]{:S(2)}) collective-permute-start(bf16[384,128]{1,0:T(8,128)(2,1)S(1)} %get-tuple-element.27.refs_0_), channel_id=1, source_target_pairs={{0,8},{8,0},{16,24},{24,16},{1,9},{9,1},{17,25},{25,17},{2,10},{10... | collective-permute-start | bytes 294920 | tf_op jit(solution)/shard_map/ppermute | solution.py:37
  34.0 2.7 %collective-permute-done.6.refs_3_ = bf16[384,128]{1,0:T(8,128)(2,1)S(1)} collective-permute-done((bf16[384,128]{1,0:T(8,128)(2,1)S(1)}, bf16[384,128]{1,0:T(8,128)(2,1)S(1)}, u32[]{:S(2)}, u32[]{:S(2)}) %collective-permute-start.6) | collective-permute-done | bytes 98336 | tf_op jit(solution)/shard_map/ppermute | solution.py:37
  36.8 1.0 %collective-permute-done.5.refs_2_ = bf16[384,128]{1,0:T(8,128)(2,1)S(1)} collective-permute-done((bf16[384,128]{1,0:T(8,128)(2,1)S(1)}, bf16[384,128]{1,0:T(8,128)(2,1)S(1)}, u32[]{:S(2)}, u32[]{:S(2)}) %collective-permute-start.5) | collective-permute-done | bytes 98336 | tf_op jit(solution)/shard_map/ppermute | solution.py:37
  37.8 0.3 collective-permute-done.4.refs_1_
  38.1 0.7 %merge_grp0.1 = (bf16[128,128]{1,0:T(8,128)(2,1)S(1)}, bf16[2,128,128]{2,1,0:T(8,128)(2,1)S(1)}) custom-call(bf16[384,128]{1,0:T(8,128)(2,1)S(1)} %get-tuple-element.27.refs_0_, bf16[384,128]{1,0:T(8,128)(2,1)S(1)} %collective-permute-done.4.refs_1_, bf16[384,128]{1,0:T(8,128)(2,1)S(1)} %collective-permute-done.5.refs_2_, ...), custom_call_target="tpu_custom_call" | custom-call | flops 83886080 | bytes 327680 | tf_op jit(solution)/shard_map/merge_grp0/pallas_call | solution.py:311
  38.8 2.6 %collective-permute-start.10 = (bf16[128,128]{1,0:T(8,128)(2,1)S(1)}, bf16[128,128]{1,0:T(8,128)(2,1)S(1)}, u32[]{:S(2)}, u32[]{:S(2)}) collective-permute-start(bf16[128,128]{1,0:T(8,128)(2,1)S(1)} %get-tuple-element.30.refs_0_), channel_id=1, source_target_pairs={{0,6},{1,7},{2,4},{3,5},{4,2},{5,3},{6,0},{7,1},{8,14},{9,15},{10,... | collective-permute-start | bytes 98312 | tf_op jit(solution)/shard_map/ppermute | solution.py:37
  41.5 0.6 %collective-permute-start.9 = (bf16[128,128]{1,0:T(8,128)(2,1)S(1)}, bf16[128,128]{1,0:T(8,128)(2,1)S(1)}, u32[]{:S(2)}, u32[]{:S(2)}) collective-permute-start(bf16[128,128]{1,0:T(8,128)(2,1)S(1)} %get-tuple-element.30.refs_0_), channel_id=1, source_target_pairs={{0,4},{1,5},{2,6},{3,7},{4,0},{5,1},{6,2},{7,3},{8,12},{9,13},{10,... | collective-permute-start | bytes 98312 | tf_op jit(solution)/shard_map/ppermute | solution.py:37
  42.1 1.2 %collective-permute-start.8 = (bf16[128,128]{1,0:T(8,128)(2,1)S(1)}, bf16[128,128]{1,0:T(8,128)(2,1)S(1)}, u32[]{:S(2)}, u32[]{:S(2)}) collective-permute-start(bf16[128,128]{1,0:T(8,128)(2,1)S(1)} %get-tuple-element.30.refs_0_), channel_id=1, source_target_pairs={{0,2},{1,3},{2,0},{3,1},{4,6},{5,7},{6,4},{7,5},{8,10},{9,11},{10,... | collective-permute-start | bytes 98312 | tf_op jit(solution)/shard_map/ppermute | solution.py:37
  43.3 0.6 %down_pass.1.own = bf16[128,128]{1,0:T(8,128)(2,1)S(1)} custom-call(bf16[2,128,128]{2,1,0:T(8,128)(2,1)S(1)} %get-tuple-element.26.refs_0_, bf16[2,128,128]{2,1,0:T(8,128)(2,1)S(1)} %get-tuple-element.28.refs_1_, bf16[3,6,128,128]{3,2,1,0:T(8,128)(2,1)S(1)} %copy-done, bf16[3,6,128,128]{3,2,1,0:T(8,128)(2,1)S(1)} %copy-done.1), custom_call_target="tpu_custom_call" | custom-call | flops 41943040 | bytes 327680 | tf_op jit(solution)/shard_map/down_pass/pallas_call | solution.py:346
  43.9 0.1 collective-permute-start.7
  44.0 0.7 %collective-permute-done.10.refs_3_ = bf16[128,128]{1,0:T(8,128)(2,1)S(1)} collective-permute-done((bf16[128,128]{1,0:T(8,128)(2,1)S(1)}, bf16[128,128]{1,0:T(8,128)(2,1)S(1)}, u32[]{:S(2)}, u32[]{:S(2)}) %collective-permute-start.10) | collective-permute-done | bytes 32800 | tf_op jit(solution)/shard_map/ppermute | solution.py:37
  44.6 2.0 %collective-permute-done.9.refs_2_ = bf16[128,128]{1,0:T(8,128)(2,1)S(1)} collective-permute-done((bf16[128,128]{1,0:T(8,128)(2,1)S(1)}, bf16[128,128]{1,0:T(8,128)(2,1)S(1)}, u32[]{:S(2)}, u32[]{:S(2)}) %collective-permute-start.9) | collective-permute-done | bytes 32800 | tf_op jit(solution)/shard_map/ppermute | solution.py:37
  46.7 0.1 collective-permute-start.11
  46.8 0.0 copy-start.8
  46.8 1.1 %copy-done.8 = bf16[1536,256]{1,0:T(8,128)(2,1)S(1)} copy-done((bf16[1536,256]{1,0:T(8,128)(2,1)S(1)}, bf16[1536,256]{1,0:T(8,128)(2,1)}, u32[]{:S(2)}) %copy-start.8) | copy-done | bytes 786456
  47.9 3.2 %image.1 = bf16[1536,256]{1,0:T(8,128)(2,1)} custom-call(f32[1]{0:T(128)S(6)} %copy.13.ridge_ref, s32[1,1536]{1,0:T(1,128)S(1)} %copy-done.7, bf16[128,128]{1,0:T(8,128)(2,1)S(1)} %down_pass.1.own, bf16[128,128]{1,0:T(8,128)(2,1)S(1)} %collective-permute-done.7.other, bf16[1920,128]{1,0:T(8,128)(2,1)S(1)} %collective-permute-done.got, ...), custom_call_target="tpu_custom_call" | custom-call | flops 1207959552 | bytes 2359296 | tf_op jit(solution)/shard_map/image/pallas_call | solution.py:381
  51.2 0.8 %finish.1 = (f32[256,256]{1,0:T(8,128)}, f32[256,256]{1,0:T(8,128)}) custom-call(bf16[512,128]{1,0:T(8,128)(2,1)S(1)} %join.1.own, bf16[512,128]{1,0:T(8,128)(2,1)S(1)} %collective-permute-done.11.other), custom_call_target="tpu_custom_call" | custom-call | tf_op jit(solution)/shard_map/finish/pallas_call | solution.py:427
  (18 shorter events, 0.1 us)
Async XLA Ops:
  1.3 28.6 %copy-start = (bf16[3,6,128,128]{3,2,1,0:T(8,128)(2,1)S(1)}, bf16[3,6,128,128]{3,2,1,0:T(8,128)(2,1)}, u32[]{:S(2)}) copy-start(bf16[3,6,128,128]{3,2,1,0:T(8,128)(2,1)} %refs_2_.1) | copy-start | bytes 1769476
  1.3 36.8 %copy-start.1 = (bf16[3,6,128,128]{3,2,1,0:T(8,128)(2,1)S(1)}, bf16[3,6,128,128]{3,2,1,0:T(8,128)(2,1)}, u32[]{:S(2)}) copy-start(bf16[3,6,128,128]{3,2,1,0:T(8,128)(2,1)} %refs_3_.1) | copy-start | bytes 1769476
  1.3 45.5 %copy-start.4 = (bf16[1536,256]{1,0:T(8,128)(2,1)S(1)}, bf16[1536,256]{1,0:T(8,128)(2,1)}, u32[]{:S(2)}) copy-start(bf16[1536,256]{1,0:T(8,128)(2,1)} %d.1) | copy-start | bytes 2359300
  1.3 45.5 %copy-start.5 = (bf16[1,1536,128]{2,1,0:T(8,128)(2,1)S(1)}, bf16[1,1536,128]{2,1,0:T(8,128)(2,1)}, u32[]{:S(2)}) copy-start(bf16[1,1536,128]{2,1,0:T(8,128)(2,1)} %down.1) | copy-start | bytes 1179652
  1.3 45.5 %copy-start.6 = (bf16[3,1,128,128]{3,2,1,0:T(8,128)(2,1)S(1)}, bf16[3,1,128,128]{3,2,1,0:T(8,128)(2,1)}, u32[]{:S(2)}) copy-start(bf16[3,1,128,128]{3,2,1,0:T(8,128)(2,1)} %ops.1) | copy-start | bytes 294916
  1.3 45.5 %copy-start.7 = (s32[1,1536]{1,0:T(1,128)S(1)}, s32[1,1536]{1,0:T(1,128)}, u32[]{:S(2)}) copy-start(s32[1,1536]{1,0:T(1,128)} %order.1) | copy-start | bytes 18436
  11.7 2.3 %collective-permute-start = (bf16[1920,128]{1,0:T(8,128)(2,1)}, bf16[1920,128]{1,0:T(8,128)(2,1)S(1)}, u32[]{:S(2)}, u32[]{:S(2)}) collective-permute-start(bf16[1920,128]{1,0:T(8,128)(2,1)} %get-tuple-element.18), channel_id=1, source_target_pairs={{0,1},{1,0},{2,3},{3,2},{4,5},{5,4},{6,7},{7,6},{8,9},{9,8},{10,11... | collective-permute-start | bytes 1474568 | tf_op jit(solution)/shard_map/ppermute | solution.py:37
  14.0 1.0 %copy-start.2 = (bf16[1280,128]{1,0:T(8,128)(2,1)S(1)}, bf16[1280,128]{1,0:T(8,128)(2,1)}, u32[]{:S(2)}) copy-start(bf16[1280,128]{1,0:T(8,128)(2,1)} %get-tuple-element.19.keep) | copy-start | bytes 983044
  14.9 0.9 %copy-start.3 = (f32[512,128]{1,0:T(8,128)S(1)}, f32[512,128]{1,0:T(8,128)}, u32[]{:S(2)}) copy-start(f32[512,128]{1,0:T(8,128)} %get-tuple-element.20.gown) | copy-start | bytes 786436
  16.2 6.1 %collective-permute-start.1 = (bf16[384,128]{1,0:T(8,128)(2,1)S(1)}, bf16[384,128]{1,0:T(8,128)(2,1)S(1)}, u32[]{:S(2)}, u32[]{:S(2)}) collective-permute-start(bf16[384,128]{1,0:T(8,128)(2,1)S(1)} %get-tuple-element.22), channel_id=1, source_target_pairs={{0,2},{1,3},{2,0},{3,1},{4,6},{5,7},{6,4},{7,5},{8,10},{9,11},{10,... | collective-permute-start | bytes 294920 | tf_op jit(solution)/shard_map/ppermute | solution.py:37
  19.2 10.7 %collective-permute-start.2 = (bf16[384,128]{1,0:T(8,128)(2,1)S(1)}, bf16[384,128]{1,0:T(8,128)(2,1)S(1)}, u32[]{:S(2)}, u32[]{:S(2)}) collective-permute-start(bf16[384,128]{1,0:T(8,128)(2,1)S(1)} %get-tuple-element.23), channel_id=1, source_target_pairs={{0,4},{1,5},{2,6},{3,7},{4,0},{5,1},{6,2},{7,3},{8,12},{9,13},{10,... | collective-permute-start | bytes 294920 | tf_op jit(solution)/shard_map/ppermute | solution.py:37
  21.8 8.1 %collective-permute-start.3 = (bf16[384,128]{1,0:T(8,128)(2,1)S(1)}, bf16[384,128]{1,0:T(8,128)(2,1)S(1)}, u32[]{:S(2)}, u32[]{:S(2)}) collective-permute-start(bf16[384,128]{1,0:T(8,128)(2,1)S(1)} %get-tuple-element.24), channel_id=1, source_target_pairs={{0,6},{1,7},{2,4},{3,5},{4,2},{5,3},{6,0},{7,1},{8,14},{9,15},{10,... | collective-permute-start | bytes 294920 | tf_op jit(solution)/shard_map/ppermute | solution.py:37
  30.5 6.3 %collective-permute-start.6 = (bf16[384,128]{1,0:T(8,128)(2,1)S(1)}, bf16[384,128]{1,0:T(8,128)(2,1)S(1)}, u32[]{:S(2)}, u32[]{:S(2)}) collective-permute-start(bf16[384,128]{1,0:T(8,128)(2,1)S(1)} %get-tuple-element.27.refs_0_), channel_id=1, source_target_pairs={{0,24},{8,16},{16,8},{24,0},{1,25},{9,17},{17,9},{25,1},{2,26},{10... | collective-permute-start | bytes 294920 | tf_op jit(solution)/shard_map/ppermute | solution.py:37
  33.0 4.8 %collective-permute-start.5 = (bf16[384,128]{1,0:T(8,128)(2,1)S(1)}, bf16[384,128]{1,0:T(8,128)(2,1)S(1)}, u32[]{:S(2)}, u32[]{:S(2)}) collective-permute-start(bf16[384,128]{1,0:T(8,128)(2,1)S(1)} %get-tuple-element.27.refs_0_), channel_id=1, source_target_pairs={{0,16},{8,24},{16,0},{24,8},{1,17},{9,25},{17,1},{25,9},{2,18},{10... | collective-permute-start | bytes 294920 | tf_op jit(solution)/shard_map/ppermute | solution.py:37
  33.5 4.6 %collective-permute-start.4 = (bf16[384,128]{1,0:T(8,128)(2,1)S(1)}, bf16[384,128]{1,0:T(8,128)(2,1)S(1)}, u32[]{:S(2)}, u32[]{:S(2)}) collective-permute-start(bf16[384,128]{1,0:T(8,128)(2,1)S(1)} %get-tuple-element.27.refs_0_), channel_id=1, source_target_pairs={{0,8},{8,0},{16,24},{24,16},{1,9},{9,1},{17,25},{25,17},{2,10},{10... | collective-permute-start | bytes 294920 | tf_op jit(solution)/shard_map/ppermute | solution.py:37
  38.8 5.8 %collective-permute-start.10 = (bf16[128,128]{1,0:T(8,128)(2,1)S(1)}, bf16[128,128]{1,0:T(8,128)(2,1)S(1)}, u32[]{:S(2)}, u32[]{:S(2)}) collective-permute-start(bf16[128,128]{1,0:T(8,128)(2,1)S(1)} %get-tuple-element.30.refs_0_), channel_id=1, source_target_pairs={{0,6},{1,7},{2,4},{3,5},{4,2},{5,3},{6,0},{7,1},{8,14},{9,15},{10,... | collective-permute-start | bytes 98312 | tf_op jit(solution)/shard_map/ppermute | solution.py:37
  41.5 5.2 %collective-permute-start.9 = (bf16[128,128]{1,0:T(8,128)(2,1)S(1)}, bf16[128,128]{1,0:T(8,128)(2,1)S(1)}, u32[]{:S(2)}, u32[]{:S(2)}) collective-permute-start(bf16[128,128]{1,0:T(8,128)(2,1)S(1)} %get-tuple-element.30.refs_0_), channel_id=1, source_target_pairs={{0,4},{1,5},{2,6},{3,7},{4,0},{5,1},{6,2},{7,3},{8,12},{9,13},{10,... | collective-permute-start | bytes 98312 | tf_op jit(solution)/shard_map/ppermute | solution.py:37
  42.1 4.6 %collective-permute-start.8 = (bf16[128,128]{1,0:T(8,128)(2,1)S(1)}, bf16[128,128]{1,0:T(8,128)(2,1)S(1)}, u32[]{:S(2)}, u32[]{:S(2)}) collective-permute-start(bf16[128,128]{1,0:T(8,128)(2,1)S(1)} %get-tuple-element.30.refs_0_), channel_id=1, source_target_pairs={{0,2},{1,3},{2,0},{3,1},{4,6},{5,7},{6,4},{7,5},{8,10},{9,11},{10,... | collective-permute-start | bytes 98312 | tf_op jit(solution)/shard_map/ppermute | solution.py:37
  43.9 2.9 %collective-permute-start.7 = (bf16[128,128]{1,0:T(8,128)(2,1)S(1)}, bf16[128,128]{1,0:T(8,128)(2,1)S(1)}, u32[]{:S(2)}, u32[]{:S(2)}) collective-permute-start(bf16[128,128]{1,0:T(8,128)(2,1)S(1)} %down_pass.1.own), channel_id=1, source_target_pairs={{0,1},{1,0},{2,3},{3,2},{4,5},{5,4},{6,7},{7,6},{8,9},{9,8},{10,11... | collective-permute-start | bytes 98312 | tf_op jit(solution)/shard_map/ppermute | solution.py:37
  46.7 4.5 %collective-permute-start.11 = (bf16[512,128]{1,0:T(8,128)(2,1)S(1)}, bf16[512,128]{1,0:T(8,128)(2,1)S(1)}, u32[]{:S(2)}, u32[]{:S(2)}) collective-permute-start(bf16[512,128]{1,0:T(8,128)(2,1)S(1)} %join.1.own), channel_id=1, source_target_pairs={{0,1},{1,0},{2,3},{3,2},{4,5},{5,4},{6,7},{7,6},{8,9},{9,8},{10,11... | collective-permute-start | bytes 393224 | tf_op jit(solution)/shard_map/ppermute | solution.py:37
  46.8 1.1 %copy-start.8 = (bf16[1536,256]{1,0:T(8,128)(2,1)S(1)}, bf16[1536,256]{1,0:T(8,128)(2,1)}, u32[]{:S(2)}) copy-start(bf16[1536,256]{1,0:T(8,128)(2,1)} %get-tuple-element.29.dense) | copy-start | bytes 2359300
